TPU v7x, 32 devices: a whole 2x2x4 slice. The times are simulated.
32 devices in a mesh: ctx: 16 (over z, y, x), wt: 2 (over core).
Axes of the slice: x: 2, y: 2, z: 4, core: 2. Of those that a mesh axis runs over, the one named last changes fastest.
Arguments:
- layer_input: bfloat16 [2048, 2048], P('ctx'), may hold values from -6 to 6
- block_table: int32 [16, 2], replicated, may hold values from 0 to 31, as said below
- routes: int32 [2048, 6], P('ctx'), may hold values from 0 to 15, all different within a row; in each aligned block of 128 rows (0 to 127, 128 to 255, ...) at most 64 rows name the same one
- grad_output: bfloat16 [2048, 2048], P('ctx'), may hold values from -6 to 6
- norm1_gain: bfloat16 [2048], P('ctx'), may hold values from 0.5 to 1.5
- query_down_weight: bfloat16 [2048, 1536], P('ctx'), may hold values from -0.125 to 0.125
- q_gain: bfloat16 [1536], P('ctx'), may hold values from 0.5 to 1.5
- q_up: bfloat16 [1536, 3072], P('ctx', 'wt'), may hold values from -0.15625 to 0.15625
- kv_down: bfloat16 [2048, 576], P('ctx'), may hold values from -0.125 to 0.125
- kv_gain: bfloat16 [512], P('ctx'), may hold values from 0.5 to 1.5
- kv_up: bfloat16 [512, 4096], P('ctx', 'wt'), may hold values from -0.25 to 0.25
- out_proj: bfloat16 [2048, 2048], P('ctx', 'wt'), may hold values from -0.375 to 0.375
- norm2_gain: bfloat16 [2048], P('ctx'), may hold values from 0.5 to 1.5
- router: bfloat16 [2048, 16], P('ctx'), may hold values from -0.125 to 0.125
- shared_gate: bfloat16 [2048, 2816], P('ctx', 'wt'), may hold values from -0.125 to 0.125
- shared_up: bfloat16 [2048, 2816], P('ctx', 'wt'), may hold values from -0.125 to 0.125
- shared_down: bfloat16 [2048, 2816], P('ctx', 'wt'), may hold values from -0.109375 to 0.109375
- expert_gate: bfloat16 [16, 2048, 1408], P('ctx', None, 'wt'), may hold values from -0.125 to 0.125
- routed_expert_up_weight: bfloat16 [16, 2048, 1408], P('ctx', None, 'wt'), may hold values from -0.125 to 0.125
- expert_down: bfloat16 [16, 1408, 2048], P('ctx', 'wt'), may hold values from -0.15625 to 0.15625
Outputs:
- output: bfloat16 [2048, 2048], P('ctx')
- grad_input: float32 [2048, 2048], P('ctx')
- grad_norm1_gain: float32 [2048], P('ctx')
- grad_query_down_weight: float32 [2048, 1536], P('ctx')
- grad_q_gain: float32 [1536], P('ctx')
- grad_q_up: float32 [1536, 3072], P('ctx', 'wt')
- grad_kv_down: float32 [2048, 576], P('ctx')
- grad_kv_gain: float32 [512], P('ctx')
- grad_kv_up: float32 [512, 4096], P('ctx', 'wt')
- grad_out_proj: float32 [2048, 2048], P('ctx', 'wt')
- grad_norm2_gain: float32 [2048], P('ctx')
- grad_router: float32 [2048, 16], P('ctx')
- grad_shared_gate: float32 [2048, 2816], P('ctx', 'wt')
- grad_shared_up: float32 [2048, 2816], P('ctx', 'wt')
- grad_shared_down: float32 [2048, 2816], P('ctx', 'wt')
- grad_expert_gate: float32 [16, 2048, 1408], P('ctx', None, 'wt')
- grad_expert_up: float32 [16, 2048, 1408], P('ctx', None, 'wt')
- grad_expert_down: float32 [16, 1408, 2048], P('ctx', 'wt')
Inputs may be any that keep to these rules, and one draw needn't show every extreme that they name: `block_table`: row i holds (b, 31 - b), and every b of 0 to 15 stands in exactly one row. `routes`: each row names 6 different experts. In the rows of one device (aligned blocks of 128 rows) no expert is named by more than 64 rows, and in some block one expert is named by exactly 64.
All inputs are finite; a program needn't handle non-finite values.
Results may differ from a plain program's by a relative error of at most 0.02.
Values may be sent and summed in bfloat16 or wider, within the bound.
No kernel may reach another device: no remote copies, remote signals or barrier semaphores. Data moves between devices by JAX's collectives and lax.ppermute only.
A program may use at most 384 MiB of HBM per device.

v0:
```python
import math

import jax
import jax.numpy as jnp
from jax import lax
from jax.sharding import PartitionSpec as P


NOPE = 128
ROPE = 64
VDIM = 128
BLOCK = 64

rms_epsilon = 1e-06
rope_base = 50000.0
route_scale = 2.446


F32 = jnp.float32
BF16 = jnp.bfloat16


def dot(left_mat, right_mat):
    return lax.dot_general(
        left_mat, right_mat, (((1,), (0,)), ((), ())), preferred_element_type=F32
    )


def dot_rows(left_mat, right_mat):
    return lax.dot_general(
        left_mat, right_mat, (((1,), (1,)), ((), ())), preferred_element_type=F32
    )


def dot_cols(left_mat, right_mat):
    return lax.dot_general(
        left_mat, right_mat, (((0,), (0,)), ((), ())), preferred_element_type=F32
    )


def normalize(values, weights):
    inverse = lax.rsqrt(jnp.mean(values * values, axis=-1, keepdims=True) + rms_epsilon)
    return (values * inverse * weights, inverse)


def norm_backward(upstream, values, inverse, weights):
    unit_rows = values * inverse
    scaled = upstream * weights
    inner_mean = jnp.mean(scaled * unit_rows, axis=-1, keepdims=True)
    return (inverse * (scaled - unit_rows * inner_mean), jnp.sum(upstream * unit_rows, axis=0))


def rope_tables(positions):
    half_dim = ROPE // 2
    exponent = jnp.arange(half_dim, dtype=F32) * (2.0 / ROPE)
    frequency = jnp.exp(-exponent * math.log(rope_base))
    angles = positions.astype(F32)[:, None] * frequency[None, :]
    return (jnp.cos(angles), jnp.sin(angles))


def rotate(values, cosine, sine_part):
    half_dim = values.shape[-1] // 2
    first_half = values[..., :half_dim]
    second_half = values[..., half_dim:]
    return jnp.concatenate(
        [
            first_half * cosine - second_half * sine_part,
            first_half * sine_part + second_half * cosine,
        ],
        axis=-1,
    )


def unrotate(values, cosine, sine_part):
    return rotate(values, cosine, -sine_part)


def silu_parts(values):
    sigma = jax.nn.sigmoid(values)
    return (values * sigma, sigma * (1.0 + values * (1.0 - sigma)))


def positions_of(table_rows):
    offsets = jnp.arange(BLOCK, dtype=jnp.int32)
    return (table_rows[:, :, None] * BLOCK + offsets[None, None, :]).reshape(-1)


CTX = ("line", "plane")


def exchange(blocks, axes=CTX):
    return lax.all_to_all(blocks, axes, split_axis=0, concat_axis=0, tiled=True)


def wt_sum(values):
    return values + other_wt(values)


def other_wt(values):
    return lax.ppermute(values, "wt", [(0, 1), (1, 0)])


def layer(
    layer_input,
    block_table,
    routes,
    grad_output,
    norm1_gain,
    query_down_weight,
    q_gain,
    q_up,
    kv_down,
    kv_gain,
    kv_up,
    out_proj,
    norm2_gain,
    router,
    shared_gate,
    shared_up,
    shared_down,
    expert_gate,
    routed_expert_up_weight,
    expert_down,
):
    n = lax.axis_size(CTX)
    wt = lax.axis_size("wt")
    c = lax.axis_index(CTX)
    w = lax.axis_index("wt")
    rows, width = layer_input.shape
    tokens = n * rows
    kvr = kv_gain.shape[0] * n
    qr = q_gain.shape[0] * n
    head_dim = NOPE + ROPE
    heads = q_up.shape[1] // head_dim
    group = lax.axis_size("plane")
    groups = lax.axis_size("line")
    own_heads = heads // group
    g = lax.axis_index("plane")
    experts = router.shape[1]
    own_d = norm1_gain.shape[0]
    own_q = q_gain.shape[0]
    latents = qr + kvr + ROPE
    score_scale = head_dim ** (-0.5)

    def half_rows(values):
        size = values.shape[0] // wt
        return lax.dynamic_slice_in_dim(values, w * size, size, 0)

    def gather_rows(values):
        return lax.all_gather(half_rows(values), CTX + ("wt",), axis=0, tiled=True)

    def gather_tokens(mine):
        return lax.all_gather(mine, ("plane", "wt", "line"), axis=0, tiled=True)

    def scatter_tokens(values, beside=()):
        some = lax.psum_scatter(values, ("plane", "wt"), scatter_dimension=0, tiled=True)
        some, beside = lax.optimization_barrier((some, beside))
        return lax.psum_scatter(some, "line", scatter_dimension=0, tiled=True), beside

    def both_halves(mine, axis):
        theirs = other_wt(mine)
        first, second = jnp.where(w == 0, mine, theirs), jnp.where(w == 0, theirs, mine)
        return jnp.concatenate([first, second], axis=axis)

    def group_moves(k):
        return [(i, i ^ k) for i in range(group)]

    def group_sum(values):
        cols = values.shape[1] // 2
        sent = lax.dynamic_slice_in_dim(values, (1 - w) * cols, cols, 1).astype(BF16)
        total = lax.dynamic_slice_in_dim(values, w * cols, cols, 1)
        total = (total + other_wt(sent).astype(F32)).reshape(group, rows, cols)
        own = lax.dynamic_index_in_dim(total, g, 0, keepdims=False)
        for k in range(1, group):
            block = lax.dynamic_index_in_dim(total, g ^ k, 0, keepdims=False).astype(BF16)
            own = own + lax.ppermute(block, "plane", group_moves(k)).astype(F32)
        return both_halves(own, 1)

    def group_gather(values):
        cols = values.shape[1] // 2
        mine = lax.dynamic_slice_in_dim(values, w * cols, cols, 1)
        out = jnp.zeros((group, rows, cols), values.dtype)
        out = lax.dynamic_update_index_in_dim(out, mine, g, 0)
        for k in range(1, group):
            got = lax.ppermute(mine, "plane", group_moves(k))
            out = lax.dynamic_update_index_in_dim(out, got, g ^ k, 0)
        return both_halves(out.reshape(group * rows, cols), 1)

    def own_group(values):
        start = lax.axis_index("line") * group * rows
        return lax.dynamic_slice_in_dim(values, start, group * rows, 0)

    lanes = 128

    def to_head_group(values):
        depth = values.shape[1] // group
        blocks = jnp.transpose(values.reshape(values.shape[0], group, depth), (1, 0, 2))
        blocks = jnp.broadcast_to(blocks[None], (groups,) + blocks.shape)
        return exchange(blocks.reshape((n,) + blocks.shape[2:])).reshape(-1, depth)

    def from_head_groups(terms):
        packed, shapes = [], []
        for values in terms:
            k, depth = values.shape[0] // n, values.shape[1]
            split = values.astype(BF16).reshape(groups, group, k, depth // lanes, lanes)
            split = jnp.transpose(split, (0, 1, 3, 2, 4))
            packed.append(split.reshape(groups, group, -1, lanes))
            shapes.append((k, depth // lanes))
        packed = jnp.concatenate(packed, axis=2)
        summed = lax.psum_scatter(
            packed.reshape(-1, lanes), "line", scatter_dimension=0, tiled=True
        )
        got = exchange(summed.reshape(group, -1, lanes), "plane")

        def finish(got):
            out, at = [], 0
            for k, blocks in shapes:
                part = got[:, at : at + k * blocks].reshape(group, blocks, k, lanes)
                out.append(jnp.transpose(part, (2, 0, 1, 3)).reshape(k, -1).astype(F32))
                at += k * blocks
            return out

        return got, finish

    gains = exchange(
        jnp.broadcast_to(
            jnp.concatenate([norm1_gain, norm2_gain, q_gain, kv_gain])[None],
            (n, 2 * own_d + q_gain.shape[0] + kv_gain.shape[0]),
        )
    )
    pad = -(latents + experts) % 128
    down_own = jnp.concatenate(
        [query_down_weight, kv_down, router, jnp.zeros((own_d, pad), BF16)], axis=1
    )
    if rows == own_d:
        gathered = (gather_rows(jnp.concatenate([layer_input, down_own], axis=1)),)
    else:
        gathered = (gather_rows(layer_input), gather_rows(down_own))
    ff_own = shared_gate.shape[1] // n
    shared_stack = jnp.stack([shared_gate, shared_up, shared_down], axis=0)
    shared_blocks = jnp.transpose(shared_stack.reshape(3, own_d, n, ff_own), (2, 0, 3, 1))
    gathered, kv_up_heads, q_up_heads, out_heads, gains, late = lax.optimization_barrier(
        (
            gathered,
            to_head_group(kv_up),
            to_head_group(q_up),
            to_head_group(out_proj),
            gains,
            (half_rows(grad_output), shared_blocks),
        )
    )
    go_half, shared_late = late
    go_all = gather_tokens(go_half)
    shared_got = exchange(shared_late)
    if rows == own_d:
        x_all, down_all = gathered[0][:, :width], gathered[0][:, width:]
    else:
        x_all, down_all = gathered
    q_down_all = down_all[:, :qr]
    kv_down_all = down_all[:, qr:latents]
    router_all = down_all[:, latents : latents + experts]
    norm1_full = gains[:, :own_d].reshape(-1).astype(F32)
    norm2_full = gains[:, own_d : 2 * own_d].reshape(-1).astype(F32)
    qgain_full = gains[:, 2 * own_d : 2 * own_d + own_q].reshape(-1).astype(F32)
    kvgain_full = gains[:, 2 * own_d + own_q :].reshape(-1).astype(F32)

    key_positions = positions_of(block_table)
    query_positions = own_group(key_positions)
    own_positions = positions_of(lax.dynamic_slice_in_dim(block_table, c, 1, 0))
    cosine_all, sine_all = rope_tables(key_positions)
    cosine_group, sine_group = rope_tables(query_positions)
    cosine, sine = rope_tables(own_positions)

    normed_all = lax.optimization_barrier(
        normalize(x_all.astype(F32), norm1_full)[0].astype(BF16)
    )
    kv_latent_all = dot(normed_all, kv_down_all)
    latent_all = normalize(kv_latent_all[:, :kvr], kvgain_full)[0].astype(BF16)
    rope_all = rotate(kv_latent_all[:, kvr:], cosine_all, sine_all).astype(BF16)
    q_normed_group = normalize(dot(own_group(normed_all), q_down_all), qgain_full)[0].astype(BF16)
    query_f = dot(q_normed_group, q_up_heads)
    key_values = dot(latent_all, kv_up_heads).astype(BF16)
    allowed = query_positions[:, None] >= key_positions[None, :]
    queries, keys, values_heads, exacts, attended = [], [], [], [], []
    for h in range(own_heads):
        query_h = query_f[:, h * head_dim : (h + 1) * head_dim]
        query_h = jnp.concatenate(
            [query_h[:, :NOPE], rotate(query_h[:, NOPE:], cosine_group, sine_group)], axis=-1
        ).astype(BF16)
        kv_h = key_values[:, h * (NOPE + VDIM) : (h + 1) * (NOPE + VDIM)]
        keys_h = jnp.concatenate([kv_h[:, :NOPE], rope_all], axis=-1)
        scores = dot_rows(query_h, keys_h) * score_scale
        log_total = jnp.log(
            jnp.sum(jnp.where(allowed, jnp.exp(scores), 0.0), axis=-1, keepdims=True)
        )
        exact = jnp.where(allowed, jnp.exp(scores - log_total), 0.0)
        queries.append(query_h)
        keys.append(keys_h)
        values_heads.append(kv_h[:, NOPE:])
        exacts.append(exact)
        attended.append(dot(exact.astype(BF16), kv_h[:, NOPE:]).astype(BF16))
    attention = jnp.concatenate(attended, axis=1)
    attention, shared_got = lax.optimization_barrier((attention, shared_got))

    inputs = layer_input.astype(F32)
    hidden_one = inputs + group_sum(dot_rows(attention, out_heads))
    normed2_f, inverse_two = normalize(hidden_one, norm2_full)
    normed_two = normed2_f.astype(BF16)
    sigma = jax.nn.sigmoid(dot(normed_two, router_all))
    expert_ids = jnp.arange(experts, dtype=jnp.int32)
    picked = jnp.any(routes[..., None] == expert_ids[None, None, :], axis=1)
    chosen = jnp.where(picked, sigma, 0.0)
    chosen_total = jnp.sum(chosen, axis=-1, keepdims=True)
    gates = route_scale * chosen / chosen_total
    gates_high = gates.astype(BF16)
    gates_low = (gates - gates_high.astype(F32)).astype(BF16)
    gates_pad = jnp.zeros((rows, -2 * experts % 128), BF16)
    sent_rows = jnp.concatenate([normed_two, gates_high, gates_low, gates_pad], axis=1)
    sent_rows, go_all = lax.optimization_barrier((sent_rows, go_all))
    got_rows = gather_tokens(half_rows(sent_rows))

    e_gate, e_up = jnp.transpose(expert_gate[0]), jnp.transpose(routed_expert_up_weight[0])
    ff = e_gate.shape[0]
    ff_all = ff + ff_own
    s_gate, s_up, s_down = jnp.transpose(shared_got, (1, 2, 0, 3)).reshape(3, ff_own, width)
    mats = jnp.concatenate([e_gate, s_gate, e_up, s_up, expert_down[0], s_down], axis=0)
    back_unit = dot_rows(go_all, mats[2 * ff_all :])
    normed_f, inverse_one = normalize(inputs, norm1_full)
    normed = normed_f.astype(BF16)
    q_latent = dot(normed, q_down_all)
    q_inverse = normalize(q_latent, qgain_full)[1]
    kv_latent = dot(normed, kv_down_all)[:, :kvr]
    kv_inverse = normalize(kv_latent, kvgain_full)[1]
    normed_half = lax.dynamic_index_in_dim(
        normed_all.reshape(n, wt, rows // wt, width), w, 1, keepdims=False
    ).reshape(tokens // wt, width)
    ready = (mats, back_unit, inverse_one, q_latent, q_inverse, kv_latent, kv_inverse, normed_half)
    got_rows, ready = lax.optimization_barrier((got_rows, ready))
    mats, back_unit, inverse_one, q_latent, q_inverse, kv_latent, kv_inverse, normed_half = ready
    normed_two_all = got_rows[:, :width]
    got_gates = got_rows[:, width : width + 2 * experts].astype(F32)
    is_own = (jnp.arange(2 * experts) % experts == c)[None]
    gate_own = jnp.sum(jnp.where(is_own, got_gates, 0.0), axis=-1, keepdims=True)

    gate_pre = dot_rows(normed_two_all, mats[:ff_all])
    up_pre = dot_rows(normed_two_all, mats[ff_all : 2 * ff_all])
    act, slope = silu_parts(gate_pre)
    hidden = act * up_pre
    is_expert = (jnp.arange(ff_all) < ff)[None]
    scale = jnp.where(is_expert, gate_own, 1.0)
    hidden_scaled = (hidden * scale).astype(BF16)
    back = back_unit * scale
    d_gate = (back * up_pre * slope).astype(BF16)
    d_up = (back * act).astype(BF16)
    grad_gate_own = jnp.sum(jnp.where(is_expert, back_unit * hidden, 0.0), axis=-1)
    d_normed = dot(jnp.concatenate([d_gate, d_up], axis=1), mats[: 2 * ff_all])
    d_normed, grad_gate_own, d_gate, d_up, hidden_scaled = lax.optimization_barrier(
        (d_normed.astype(BF16), grad_gate_own, d_gate, d_up, hidden_scaled)
    )
    ffn_part = dot(hidden_scaled, mats[2 * ff_all :]).astype(BF16)
    grad_expert_gate = dot_cols(d_gate[:, :ff], normed_two_all)
    grad_expert_up = dot_cols(d_up[:, :ff], normed_two_all)
    grad_expert_down = dot_cols(hidden_scaled[:, :ff], go_all)
    grad_gates = wt_sum(grad_gate_own).reshape(group, wt, groups, rows // wt)
    grad_gates = exchange(jnp.transpose(grad_gates, (2, 0, 1, 3)).reshape(n, rows))
    grad_expert_gate = jnp.transpose(grad_expert_gate)[None]
    grad_expert_up = jnp.transpose(grad_expert_up)[None]
    grad_expert_down = grad_expert_down[None]
    d_shared_in = dot_cols(jnp.concatenate([d_gate[:, ff:], d_up[:, ff:]], axis=1), normed_two_all)
    d_shared_out = dot_cols(hidden_scaled[:, ff:], go_all)
    d_shared = jnp.concatenate([d_shared_in, d_shared_out], axis=0).astype(BF16)
    d_shared = jnp.transpose(d_shared.reshape(3, ff_own, n, own_d), (2, 0, 1, 3))
    d_shared = exchange(d_shared)
    grad_normed_half, (d_shared, grad_gates, ffn_part, grad_expert_gate) = scatter_tokens(
        d_normed, (d_shared, grad_gates, ffn_part, grad_expert_gate)
    )
    grad_normed_half, ffn_part, grad_expert_up, grad_expert_down = lax.optimization_barrier(
        (grad_normed_half, ffn_part, grad_expert_up, grad_expert_down)
    )
    ffn_half = scatter_tokens(ffn_part)[0]
    grad_normed_two = both_halves(grad_normed_half, 0).astype(F32)

    grad_gates = jnp.where(picked, jnp.transpose(grad_gates), 0.0)
    grad_chosen = (
        route_scale * grad_gates - jnp.sum(grad_gates * gates, axis=-1, keepdims=True)
    ) / chosen_total
    grad_logits = (grad_chosen * chosen * (1.0 - chosen)).astype(BF16)
    upstream = grad_output.astype(F32)
    grad_normed_two = grad_normed_two + dot_rows(grad_logits, router_all)
    grad_router_part = dot_cols(grad_logits, normed_two)
    grad_hidden, norm2_part = norm_backward(grad_normed_two, hidden_one, inverse_two, norm2_full)
    grad_hidden = grad_hidden + upstream
    grad_hidden_half = grad_hidden.astype(BF16)
    hidden_group = group_gather(grad_hidden_half)
    grad_attention = dot(hidden_group, out_heads).astype(BF16)

    query_parts, kv_parts, rope_part = [], [], 0.0
    for h in range(own_heads):
        grad_att = grad_attention[:, h * VDIM : (h + 1) * VDIM]
        delta = jnp.sum(grad_att.astype(F32) * attended[h].astype(F32), axis=-1, keepdims=True)
        grad_probs = dot_rows(grad_att, values_heads[h])
        grad_scores = (exacts[h] * (grad_probs - delta)).astype(BF16)
        grad_query = score_scale * dot(grad_scores, keys[h])
        grad_keys = score_scale * dot_cols(grad_scores, queries[h])
        grad_values = dot_cols(exacts[h].astype(BF16), grad_att)
        query_parts.append(grad_query[:, :NOPE])
        query_parts.append(unrotate(grad_query[:, NOPE:], cosine_group, sine_group))
        kv_parts.append(grad_keys[:, :NOPE])
        kv_parts.append(grad_values)
        rope_part = rope_part + grad_keys[:, NOPE:]
    grad_query_half = jnp.concatenate(query_parts, axis=-1).astype(BF16)
    grad_kv_heads = jnp.concatenate(kv_parts, axis=-1).astype(BF16)
    kv_part = jnp.concatenate([dot_rows(grad_kv_heads, kv_up_heads), rope_part], axis=1)
    kv_part = kv_part.astype(BF16).reshape(n, wt, rows // wt, kvr + ROPE)
    kv_theirs = other_wt(lax.dynamic_index_in_dim(kv_part, 1 - w, 1, keepdims=False))
    kv_part = lax.dynamic_index_in_dim(kv_part, w, 1, keepdims=False) + kv_theirs
    kv_got, grad_q_normed = lax.optimization_barrier(
        (exchange(kv_part), group_sum(dot_rows(grad_query_half, q_up_heads)))
    )
    kv_own = both_halves(jnp.sum(kv_got.astype(F32), axis=0), 0)
    weight_terms, kv_own = lax.optimization_barrier(
        (
            (
                dot_cols(hidden_group, attention).astype(BF16),
                dot_cols(q_normed_group, grad_query_half).astype(BF16),
                dot_cols(latent_all, grad_kv_heads).astype(BF16),
            ),
            kv_own,
        )
    )
    heads_back, heads_finish = from_head_groups(weight_terms)
    d_shared = jnp.transpose(d_shared, (1, 3, 0, 2)).reshape(3, own_d, n * ff_own).astype(F32)

    grad_q_latent, qgain_part = norm_backward(grad_q_normed, q_latent, q_inverse, qgain_full)
    grad_kv_part, kvgain_part = norm_backward(
        kv_own[:, :kvr], kv_latent, kv_inverse, kvgain_full
    )
    grad_rope_raw = unrotate(kv_own[:, kvr:], cosine, sine)
    grad_latents = jnp.concatenate([grad_q_latent, grad_kv_part, grad_rope_raw], axis=-1).astype(
        BF16
    )
    own_cols = -(-latents // (8 * n * wt)) * 8
    col_blocks = jnp.pad(half_rows(grad_latents), ((0, 0), (0, own_cols * n * wt - latents)))
    col_blocks = jnp.transpose(col_blocks.reshape(rows // wt, n, wt * own_cols), (1, 0, 2))
    latent_cols = exchange(col_blocks).reshape(tokens // wt, wt * own_cols)
    grad_normed = dot_rows(grad_latents, down_all[:, :latents])
    grad_input, norm1_part = norm_backward(grad_normed, inputs, inverse_one, norm1_full)
    grad_input = grad_input + grad_hidden
    down_cols = dot_cols(latent_cols, normed_half)
    down_theirs = other_wt(lax.dynamic_slice_in_dim(down_cols, (1 - w) * own_cols, own_cols, 0))
    down_cols = lax.dynamic_slice_in_dim(down_cols, w * own_cols, own_cols, 0) + down_theirs
    down_cols = jnp.transpose(down_cols.reshape(own_cols, n, own_d), (1, 0, 2))

    small = jnp.concatenate(
        [
            norm1_part.reshape(n, -1),
            norm2_part.reshape(n, -1),
            qgain_part.reshape(n, -1),
            kvgain_part.reshape(n, -1),
            jnp.transpose(grad_router_part.reshape(experts, n, own_d), (1, 0, 2)).reshape(n, -1),
        ],
        axis=1,
    )
    last = jnp.concatenate([down_cols, small.reshape(n, -1, own_d)], axis=1)
    last = exchange(last.astype(BF16))
    last, heads_back = lax.optimization_barrier((last, heads_back))
    grad_out_proj, grad_q_up, grad_kv_up = heads_finish(heads_back)
    last = last.astype(F32)
    small = jnp.sum(last[:, own_cols:], axis=0).reshape(-1)
    grad_down = both_halves(last[:, :own_cols], 1).reshape(-1, own_d)
    ffn_half = lax.optimization_barrier((ffn_half, last))[0]
    output = (hidden_one + both_halves(ffn_half, 0).astype(F32)).astype(BF16)
    edge = 2 * own_d + own_q
    edge_kv = edge + kv_gain.shape[0]
    return (
        output,
        grad_input,
        small[:own_d],
        jnp.transpose(grad_down[:qr]),
        small[2 * own_d : edge],
        grad_q_up,
        jnp.transpose(grad_down[qr:latents]),
        small[edge:edge_kv],
        grad_kv_up,
        grad_out_proj,
        small[own_d : 2 * own_d],
        jnp.transpose(small[edge_kv:].reshape(experts, own_d)),
        d_shared[0],
        d_shared[1],
        d_shared[2],
        grad_expert_gate,
        grad_expert_up,
        grad_expert_down,
    )


def solution(mesh):
    n, wt = mesh.devices.shape
    plane = math.gcd(4, n)
    mesh = jax.sharding.Mesh(
        mesh.devices.reshape(n // plane, plane, wt), CTX + ("wt",)
    )
    placed = (
        P(CTX, None),
        P(),
        P(CTX, None),
        P(CTX, None),
        P(CTX),
        P(CTX, None),
        P(CTX),
        P(CTX, "wt"),
        P(CTX, None),
        P(CTX),
        P(CTX, "wt"),
        P(CTX, "wt"),
        P(CTX),
        P(CTX, None),
        P(CTX, "wt"),
        P(CTX, "wt"),
        P(CTX, "wt"),
        P(CTX, None, "wt"),
        P(CTX, None, "wt"),
        P(CTX, "wt", None),
    )
    return jax.shard_map(
        layer,
        mesh=mesh,
        in_specs=placed,
        out_specs=(
            P(CTX, None),
            P(CTX, None),
            P(CTX),
            P(CTX, None),
            P(CTX),
            P(CTX, "wt"),
            P(CTX, None),
            P(CTX),
            P(CTX, "wt"),
            P(CTX, "wt"),
            P(CTX),
            P(CTX, None),
            P(CTX, "wt"),
            P(CTX, "wt"),
            P(CTX, "wt"),
            P(CTX, None, "wt"),
            P(CTX, None, "wt"),
            P(CTX, "wt", None),
        ),
        check_vma=False,
    )
```

profile of v0, /device:TPU:0, one launch (start us, length us, event | category | flops | bytes accessed | tf_op | source)
XLA Modules:
  0.0 756.2 jit_solution(2907294548685383853)
XLA Ops:
  14.5 8.3 %all-to-all-start.3 = ((bf16[16,2,192]{2,1,0:T(2,128)(2,1)}), bf16[16,2,192]{2,1,0:T(2,128)(2,1)S(1)}, u32[]{:S(2)}, u32[]{:S(2)}) async-start(bf16[16,2,192]{2,1,0:T(2,128)(2,1)} %reshape.508), calls=%async_computation.3 | async-start | bytes 32768 | tf_op jit(solution)/shard_map/all_to_all | solution.py:92
  22.9 7.4 all-to-all-done.3
  35.0 16.2 %all-to-all-done = bf16[16,32,512]{2,1,0:T(8,128)(2,1)S(1)} async-done(((bf16[16,32,512]{2,1,0:T(8,128)(2,1)}), bf16[16,32,512]{2,1,0:T(8,128)(2,1)S(1)}, u32[]{:S(2)}, u32[]{:S(2)}) %all-to-all-start) | async-done | bytes 524320 | tf_op jit(solution)/shard_map/all_to_all | solution.py:92
  52.4 4.4 all-to-all-start.2
  57.9 37.8 %all-to-all-done.2 = bf16[16,128,256]{2,1,0:T(8,128)(2,1)S(1)} async-done(((bf16[16,128,256]{2,1,0:T(8,128)(2,1)}), bf16[16,128,256]{2,1,0:T(8,128)(2,1)S(1)}, u32[]{:S(2)}, u32[]{:S(2)}) %all-to-all-start.2) | async-done | bytes 1048608 | tf_op jit(solution)/shard_map/all_to_all | solution.py:92
  96.9 7.2 all-to-all-start.1
  110.1 37.9 %all-to-all-done.1 = bf16[16,96,384]{2,1,0:T(8,128)(2,1)S(1)} async-done(((bf16[16,96,384]{2,1,0:T(8,128)(2,1)}), bf16[16,96,384]{2,1,0:T(8,128)(2,1)S(1)}, u32[]{:S(2)}, u32[]{:S(2)}) %all-to-all-start.1) | async-done | bytes 1179680 | tf_op jit(solution)/shard_map/all_to_all | solution.py:92
  148.0 29.1 %all-gather.4.cloned.1.call-done = bf16[2048,4224]{1,0:T(8,128)(2,1)} async-done(((bf16[64,4224]{1,0:T(8,128)(2,1)}), bf16[2048,4224]{1,0:T(8,128)(2,1)}) %all-gather.4.cloned.1.call-update) | async-done | bytes 17301520 | tf_op jit(solution)/shard_map/all_gather | solution.py:150
  177.5 5.1 fusion
  182.6 8.0 %fusion.2 = bf16[2048,2048]{1,0:T(8,128)(2,1)} fusion(f32[2048]{0:T(1024)S(1)} %get-tuple-element.312, f32[2048]{0:T(1024)S(1)} %add_rsqrt_fusion.1, bf16[2048,4224]{1,0:T(8,128)(2,1)} %all-gather.4.cloned.1.call-done), kind=kLoop, calls=%fused_computation.4 | loop fusion | flops 16777216 | bytes 16793600 | tf_op jit(solution)/shard_map/convert_element_type | solution.py:275
  192.0 4.6 all-to-all-start.4
  196.8 6.4 multiply_reduce_fusion.1
  203.2 9.5 %fusion.45 = f32[2048,576]{0,1:T(8,128)S(1)} fusion(bf16[2048,2048]{1,0:T(8,128)(2,1)} %fusion.2, bf16[2048,4224]{1,0:T(8,128)(2,1)} %all-gather.4.cloned.1.call-done), kind=kOutput, calls=%fused_computation.71 | convolution fusion | flops 4831838208 | bytes 15728640 | tf_op jit(solution)/shard_map/dot_general | solution.py:24
  224.8 5.0 all-to-all-done.4
  238.1 5.2 collective-permute-start.3
  245.7 10.5 %collective-permute-done.3 = bf16[128,1024]{1,0:T(8,128)(2,1)} collective-permute-done((bf16[128,1024]{1,0:T(8,128)(2,1)S(1)}, bf16[128,1024]{1,0:T(8,128)(2,1)}, u32[]{:S(2)}, u32[]{:S(2)}) %collective-permute-start.3) | collective-permute-done | bytes 262176 | tf_op jit(solution)/shard_map/ppermute | solution.py:176
  256.1 6.3 collective-permute-done.2
  262.4 5.9 collective-permute-done.1
  275.8 5.0 all-gather.6.cloned.1.call-done
  283.7 4.9 constant_dynamic-slice_fusion.3
  293.3 7.1 multiply_reduce_fusion.12
  300.4 4.8 multiply_reduce_fusion.7
  305.8 9.3 %fusion.33 = f32[2048,792]{0,1:T(8,128)} fusion(bf16[2048,2048]{1,0:T(8,128)(2,1)S(1)} %bitcast.227, bf16[88,2048]{1,0:T(8,128)(2,1)S(1)} %bitcast.276, bf16[704,2048]{1,0:T(8,128)(2,1)S(1)} %bitcast.255), kind=kOutput, calls=%fused_computation.50 | convolution fusion | flops 6650265600 | bytes 18120704 | tf_op jit(solution)/shard_map/dot_general | solution.py:30
  315.0 46.9 %all-gather.8.cloned.1.call-done = bf16[2048,2176]{1,0:T(8,128)(2,1)} async-done(((bf16[64,2176]{1,0:T(8,128)(2,1)}), bf16[2048,2176]{1,0:T(8,128)(2,1)}) %all-gather.8.cloned.1.call-update) | async-done | bytes 8912912 | tf_op jit(solution)/shard_map/all_gather | solution.py:153
  362.0 12.0 %fusion.21 = f32[2048,792]{0,1:T(8,128)} fusion(bf16[2048,2176]{1,0:T(8,128)(2,1)} %all-gather.8.cloned.1.call-done, bf16[2376,2048]{1,0:T(8,128)(2,1)} %copy-done.50), kind=kOutput, calls=%fused_computation.35 | convolution fusion | flops 6643777536 | bytes 18120704 | tf_op jit(solution)/shard_map/dot_general | solution.py:30
  375.2 17.6 %select_reduce_fusion = (f32[2048]{0:T(1024)S(1)}, bf16[2048,792]{0,1:T(8,128)(2,1)S(1)}, bf16[2048,792]{0,1:T(8,128)(2,1)}, bf16[2048,792]{0,1:T(8,128)(2,1)S(1)}) fusion(f32[2048,792]{0,1:T(8,128)} %fusion.33, pred[792]{0:T(1024)(128)(4,1)S(1)} %iota_compare_fusion.1, f32[2048,792]{0,1:T(8,128)} %fusion.21, f32[2048]{0:T(1024)S(1)} %select_reduce_fusion.1, ...), kind=kOutput, calls=%fused_computation.19 | convolution fusion | flops 6677837824 | bytes 34358040 | tf_op jit(solution)/shard_map/dot_general | solution.py:30
  394.6 19.5 %convolution_convert_fusion.1 = bf16[2048,2048]{1,0:T(8,128)(2,1)} fusion(bf16[2048,792]{0,1:T(8,128)(2,1)S(1)} %get-tuple-element.77, bf16[2048,792]{0,1:T(8,128)(2,1)S(1)} %get-tuple-element.76, bf16[2376,2048]{1,0:T(8,128)(2,1)} %copy-done.50), kind=kOutput, calls=%fused_computation.10 | convolution fusion | flops 13304725504 | bytes 21364736 | tf_op jit(solution)/shard_map/dot_general | solution.py:24
  415.5 5.9 fusion.47
  421.4 11.1 %fusion.30 = f32[1,2048,704]{1,2,0:T(8,128)} fusion(bf16[2048,2176]{1,0:T(8,128)(2,1)} %all-gather.8.cloned.1.call-done, bf16[2048,792]{0,1:T(8,128)(2,1)S(1)} %copy-done.107), kind=kOutput, calls=%fused_computation.46 | convolution fusion | flops 5905580032 | bytes 17039360 | tf_op jit(solution)/shard_map/dot_general | solution.py:36
  435.8 3.7 all-to-all-start.6
  441.1 5.7 all-to-all-done.6
  450.5 13.9 %convolution_convert_fusion = bf16[2048,2048]{1,0:T(8,128)(2,1)} fusion(bf16[2048,792]{0,1:T(8,128)(2,1)} %get-tuple-element.78, bf16[2376,2048]{1,0:T(8,128)(2,1)} %copy-done.50), kind=kOutput, calls=%fused_computation.9 | convolution fusion | flops 6647971840 | bytes 14876672 | tf_op jit(solution)/shard_map/dot_general | solution.py:24
  464.4 10.2 %all-to-all-done.5 = bf16[16,3,88,128]{3,2,1,0:T(8,128)(2,1)S(1)} async-done(((bf16[16,3,88,128]{3,2,1,0:T(8,128)(2,1)}), bf16[16,3,88,128]{3,2,1,0:T(8,128)(2,1)S(1)}, u32[]{:S(2)}, u32[]{:S(2)}) %all-to-all-start.5) | async-done | bytes 1081376 | tf_op jit(solution)/shard_map/all_to_all | solution.py:92
  474.6 21.4 %reduce-scatter.6.cloned.1.call-done = bf16[256,2048]{1,0:T(8,128)(2,1)} async-done(((bf16[2048,2048]{1,0:T(8,128)(2,1)}), bf16[256,2048]{1,0:T(8,128)(2,1)}) %reduce-scatter.6.cloned.1.call-update) | async-done | bytes 1048592 | tf_op jit(solution)/shard_map/reduce_scatter | solution.py:156
  496.1 11.1 %fusion.27 = f32[1,2048,704]{1,2,0:T(8,128)} fusion(bf16[2048,2176]{1,0:T(8,128)(2,1)} %all-gather.8.cloned.1.call-done, bf16[2048,792]{0,1:T(8,128)(2,1)} %copy-done.105), kind=kOutput, calls=%fused_computation.45 | convolution fusion | flops 5905580032 | bytes 17039360 | tf_op jit(solution)/shard_map/dot_general | solution.py:36
  507.3 10.1 %convolution_bitcast_fusion = f32[1,704,2048]{2,1,0:T(8,128)} fusion(bf16[2048,2048]{1,0:T(8,128)(2,1)} %all-gather.6.cloned.1.call-done, bf16[2048,792]{0,1:T(8,128)(2,1)S(1)} %copy-done.98), kind=kOutput, calls=%fused_computation.47 | convolution fusion | flops 5905580032 | bytes 17039360 | tf_op jit(solution)/shard_map/dot_general | solution.py:36
  517.4 8.1 %reduce-scatter.8.cloned.1.call-done = bf16[64,2048]{1,0:T(8,128)(2,1)} async-done(((bf16[256,2048]{1,0:T(8,128)(2,1)}), bf16[64,2048]{1,0:T(8,128)(2,1)}) %reduce-scatter.8.cloned.1.call-update) | async-done | bytes 262160 | tf_op jit(solution)/shard_map/reduce_scatter | solution.py:158
  534.5 5.7 collective-permute-done.7
  540.2 6.0 collective-permute-done.8
  582.4 3.7 all-to-all-start.7
  591.8 22.5 %collective-permute-done.15 = bf16[128,768]{1,0:T(8,128)(2,1)S(1)} collective-permute-done((bf16[128,768]{1,0:T(8,128)(2,1)S(1)}, bf16[128,768]{1,0:T(8,128)(2,1)S(1)}, u32[]{:S(2)}, u32[]{:S(2)}) %collective-permute-start.15) | collective-permute-done | bytes 196640 | tf_op jit(solution)/shard_map/ppermute | solution.py:176
  620.1 4.5 convolution_convert_fusion.10
  654.0 5.6 all-to-all-start.8
  660.0 22.5 %all-to-all-done.8 = bf16[16,64,144]{2,1,0:T(8,128)(2,1)S(1)} async-done(((bf16[16,64,144]{2,1,0:T(8,128)(2,1)}), bf16[16,64,144]{2,1,0:T(8,128)(2,1)S(1)}, u32[]{:S(2)}, u32[]{:S(2)}) %all-to-all-start.8) | async-done | bytes 294944 | tf_op jit(solution)/shard_map/all_to_all | solution.py:92
  686.5 7.5 fusion.69
  696.1 11.8 %all-to-all-start.9 = ((bf16[16,91,128]{2,1,0:T(8,128)(2,1)}), bf16[16,91,128]{2,1,0:T(8,128)(2,1)S(1)}, u32[]{:S(2)}, u32[]{:S(2)}) async-start(bf16[16,91,128]{2,1,0:T(8,128)(2,1)} %pad_maximum_fusion.13), calls=%async_computation.13 | async-start | bytes 786432 | tf_op jit(solution)/shard_map/all_to_all | solution.py:92
  721.1 4.2 all-to-all-start.10
  727.9 5.6 all-to-all-done.10
  (568 shorter events, 196.7 us)
Async XLA Ops:
  7.2 169.9 %all-gather.4.cloned.1.call-start = ((), (), s32[]{:S(2)}) async-start(), calls=%async_computation.16 | async-start | bytes 17842176 | tf_op jit(solution)/shard_map/all_gather | solution.py:150
  14.5 15.8 %all-to-all-start.3 = ((bf16[16,2,192]{2,1,0:T(2,128)(2,1)}), bf16[16,2,192]{2,1,0:T(2,128)(2,1)S(1)}, u32[]{:S(2)}, u32[]{:S(2)}) async-start(bf16[16,2,192]{2,1,0:T(2,128)(2,1)} %reshape.508), calls=%async_computation.3 | async-start | bytes 32768 | tf_op jit(solution)/shard_map/all_to_all | solution.py:92
  31.2 20.0 %all-to-all-start = ((bf16[16,32,512]{2,1,0:T(8,128)(2,1)}), bf16[16,32,512]{2,1,0:T(8,128)(2,1)S(1)}, u32[]{:S(2)}, u32[]{:S(2)}) async-start(bf16[16,32,512]{2,1,0:T(8,128)(2,1)} %bitcast.1), calls=%async_computation | async-start | bytes 1048576 | tf_op jit(solution)/shard_map/all_to_all | solution.py:92
  52.4 51.9 %copy-start.77 = (bf16[128,1408]{1,0:T(8,128)(2,1)S(1)}, bf16[128,1408]{1,0:T(8,128)(2,1)}, u32[]{:S(2)}) copy-start(bf16[128,1408]{1,0:T(8,128)(2,1)} %param.36) | copy-start | bytes 1081348
  52.4 43.4 %all-to-all-start.2 = ((bf16[16,128,256]{2,1,0:T(8,128)(2,1)}), bf16[16,128,256]{2,1,0:T(8,128)(2,1)S(1)}, u32[]{:S(2)}, u32[]{:S(2)}) async-start(bf16[16,128,256]{2,1,0:T(8,128)(2,1)} %bitcast.7), calls=%async_computation.2 | async-start | bytes 2097152 | tf_op jit(solution)/shard_map/all_to_all | solution.py:92
  56.8 48.4 %copy-start.78 = (bf16[128,1408]{1,0:T(8,128)(2,1)S(1)}, bf16[128,1408]{1,0:T(8,128)(2,1)}, u32[]{:S(2)}) copy-start(bf16[128,1408]{1,0:T(8,128)(2,1)} %param.35) | copy-start | bytes 1081348
  56.8 49.3 %copy-start.79 = (bf16[128,1408]{1,0:T(8,128)(2,1)S(1)}, bf16[128,1408]{1,0:T(8,128)(2,1)}, u32[]{:S(2)}) copy-start(bf16[128,1408]{1,0:T(8,128)(2,1)} %param.34) | copy-start | bytes 1081348
  95.7 134.0 %copy-start.27 = (bf16[16,128,256]{2,1,0:T(8,128)(2,1)}, bf16[16,128,256]{2,1,0:T(8,128)(2,1)S(1)}, u32[]{:S(2)}) copy-start(bf16[16,128,256]{2,1,0:T(8,128)(2,1)S(1)} %all-to-all-done.2) | copy-start | bytes 3145732
  96.9 80.2 %copy-start.134 = (s32[16,2]{0,1:T(2,128)S(1)}, s32[16,2]{0,1:T(2,128)}, u32[]{:S(2)}) copy-start(s32[16,2]{0,1:T(2,128)} %param.21) | copy-start | bytes 388
  96.9 51.0 %all-to-all-start.1 = ((bf16[16,96,384]{2,1,0:T(8,128)(2,1)}), bf16[16,96,384]{2,1,0:T(8,128)(2,1)S(1)}, u32[]{:S(2)}, u32[]{:S(2)}) async-start(bf16[16,96,384]{2,1,0:T(8,128)(2,1)} %bitcast.4), calls=%async_computation.1 | async-start | bytes 2359296 | tf_op jit(solution)/shard_map/all_to_all | solution.py:92
  104.2 176.6 %all-gather.6.cloned.1.call-start = ((), (), s32[]{:S(2)}) async-start(), calls=%async_computation.17 | async-start | bytes 8650752 | tf_op jit(solution)/shard_map/all_gather | solution.py:153
  148.0 65.1 %copy-start.7 = (bf16[16,96,384]{2,1,0:T(8,128)(2,1)}, bf16[16,96,384]{2,1,0:T(8,128)(2,1)S(1)}, u32[]{:S(2)}) copy-start(bf16[16,96,384]{2,1,0:T(8,128)(2,1)S(1)} %all-to-all-done.1) | copy-start | bytes 3538948
  182.6 89.4 %copy-start.89 = (f32[2048]{0:T(1024)}, f32[2048]{0:T(1024)S(1)}, u32[]{:S(2)}) copy-start(f32[2048]{0:T(1024)S(1)} %get-tuple-element.311) | copy-start | bytes 24580
  182.6 117.7 %copy-start.101 = (f32[2048]{0:T(1024)}, f32[2048]{0:T(1024)S(1)}, u32[]{:S(2)}) copy-start(f32[2048]{0:T(1024)S(1)} %get-tuple-element.312) | copy-start | bytes 24580
  192.0 37.7 %all-to-all-start.4 = ((bf16[16,3,88,128]{3,2,1,0:T(8,128)(2,1)}), bf16[16,3,88,128]{3,2,1,0:T(8,128)(2,1)S(1)}, u32[]{:S(2)}, u32[]{:S(2)}) async-start(bf16[16,3,88,128]{3,2,1,0:T(8,128)(2,1)} %copy.269), calls=%async_computation.4 | async-start | bytes 2162688 | tf_op jit(solution)/shard_map/all_to_all | solution.py:92
  196.6 165.3 %all-gather.8.cloned.1.call-start = ((), (), s32[]{:S(2)}) async-start(), calls=%async_computation.18 | async-start | bytes 9191424 | tf_op jit(solution)/shard_map/all_gather | solution.py:153
  232.9 2.9 collective-permute-start
  238.1 18.1 %collective-permute-start.3 = (bf16[128,1024]{1,0:T(8,128)(2,1)S(1)}, bf16[128,1024]{1,0:T(8,128)(2,1)}, u32[]{:S(2)}, u32[]{:S(2)}) collective-permute-start(bf16[128,1024]{1,0:T(8,128)(2,1)S(1)} %get-tuple-element.278), channel_id=1, source_target_pairs={{0,6},{2,4},{4,2},{6,0},{1,7},{3,5},{5,3},{7,1},{8,14},{10,12},{12... | collective-permute-start | bytes 786440 | tf_op jit(solution)/shard_map/ppermute | solution.py:176
  243.3 19.2 %collective-permute-start.2 = (bf16[128,1024]{1,0:T(8,128)(2,1)S(1)}, bf16[128,1024]{1,0:T(8,128)(2,1)}, u32[]{:S(2)}, u32[]{:S(2)}) collective-permute-start(bf16[128,1024]{1,0:T(8,128)(2,1)S(1)} %get-tuple-element.279), channel_id=1, source_target_pairs={{0,4},{2,6},{4,0},{6,2},{1,5},{3,7},{5,1},{7,3},{8,12},{10,14},{12... | collective-permute-start | bytes 786440 | tf_op jit(solution)/shard_map/ppermute | solution.py:176
  244.3 24.0 %collective-permute-start.1 = (bf16[128,1024]{1,0:T(8,128)(2,1)S(1)}, bf16[128,1024]{1,0:T(8,128)(2,1)}, u32[]{:S(2)}, u32[]{:S(2)}) collective-permute-start(bf16[128,1024]{1,0:T(8,128)(2,1)S(1)} %get-tuple-element.277), channel_id=1, source_target_pairs={{0,2},{2,0},{4,6},{6,4},{1,3},{3,1},{5,7},{7,5},{8,10},{10,8},{12,... | collective-permute-start | bytes 786440 | tf_op jit(solution)/shard_map/ppermute | solution.py:176
  269.6 2.0 collective-permute-start.4
  281.6 214.5 %reduce-scatter.6.cloned.1.call-start = ((), (), s32[]{:S(2)}) async-start(), calls=%async_computation.19 | async-start | bytes 9437184 | tf_op jit(solution)/shard_map/reduce_scatter | solution.py:156
  415.2 19.9 %collective-permute-start.5 = (f32[2048]{0:T(1024)S(1)}, f32[2048]{0:T(1024)S(1)}, u32[]{:S(2)}, u32[]{:S(2)}) collective-permute-start(f32[2048]{0:T(1024)S(1)} %get-tuple-element.79), channel_id=1, source_target_pairs={{0,1},{1,0},{2,3},{3,2},{4,5},{5,4},{6,7},{7,6},{8,9},{9,8},{10,11... | collective-permute-start | bytes 24584 | tf_op jit(solution)/shard_map/ppermute | solution.py:100
  435.8 10.9 %all-to-all-start.6 = ((f32[16,1,128]{2,1,0:T(1,128)}), f32[16,1,128]{2,1,0:T(1,128)S(1)}, u32[]{:S(2)}, u32[]{:S(2)}) async-start(f32[16,1,128]{2,1,0:T(1,128)} %bitcast.34), calls=%async_computation.7 | async-start | bytes 16384 | tf_op jit(solution)/shard_map/all_to_all | solution.py:92
  446.8 27.8 %all-to-all-start.5 = ((bf16[16,3,88,128]{3,2,1,0:T(8,128)(2,1)}), bf16[16,3,88,128]{3,2,1,0:T(8,128)(2,1)S(1)}, u32[]{:S(2)}, u32[]{:S(2)}) async-start(bf16[16,3,88,128]{3,2,1,0:T(8,128)(2,1)} %bitcast.220), calls=%async_computation.6 | async-start | bytes 2162688 | tf_op jit(solution)/shard_map/all_to_all | solution.py:92
  450.5 75.0 %reduce-scatter.8.cloned.1.call-start = ((), (), s32[]{:S(2)}) async-start(), calls=%async_computation.20 | async-start | bytes 1310720 | tf_op jit(solution)/shard_map/reduce_scatter | solution.py:158
  496.1 221.5 %reduce-scatter.10.cloned.1.call-start = ((), (), s32[]{:S(2)}) async-start(), calls=%async_computation.21 | async-start | bytes 9437184 | tf_op jit(solution)/shard_map/reduce_scatter | solution.py:156
  525.5 1.7 collective-permute-start.6
  531.0 9.2 %collective-permute-start.7 = (bf16[128,1024]{1,0:T(8,128)(2,1)S(1)}, bf16[128,1024]{1,0:T(8,128)(2,1)S(1)}, u32[]{:S(2)}, u32[]{:S(2)}) collective-permute-start(bf16[128,1024]{1,0:T(8,128)(2,1)S(1)} %get-tuple-element.261), channel_id=1, source_target_pairs={{0,2},{2,0},{4,6},{6,4},{1,3},{3,1},{5,7},{7,5},{8,10},{10,8},{12,... | collective-permute-start | bytes 786440 | tf_op jit(solution)/shard_map/ppermute | solution.py:185
  532.5 13.7 %collective-permute-start.8 = (bf16[128,1024]{1,0:T(8,128)(2,1)S(1)}, bf16[128,1024]{1,0:T(8,128)(2,1)S(1)}, u32[]{:S(2)}, u32[]{:S(2)}) collective-permute-start(bf16[128,1024]{1,0:T(8,128)(2,1)S(1)} %get-tuple-element.261), channel_id=1, source_target_pairs={{0,4},{2,6},{4,0},{6,2},{1,5},{3,7},{5,1},{7,3},{8,12},{10,14},{12... | collective-permute-start | bytes 786440 | tf_op jit(solution)/shard_map/ppermute | solution.py:185
  534.0 12.3 %collective-permute-start.9 = (bf16[128,1024]{1,0:T(8,128)(2,1)S(1)}, bf16[128,1024]{1,0:T(8,128)(2,1)S(1)}, u32[]{:S(2)}, u32[]{:S(2)}) collective-permute-start(bf16[128,1024]{1,0:T(8,128)(2,1)S(1)} %get-tuple-element.261), channel_id=1, source_target_pairs={{0,6},{2,4},{4,2},{6,0},{1,7},{3,5},{5,3},{7,1},{8,14},{10,12},{12... | collective-permute-start | bytes 786440 | tf_op jit(solution)/shard_map/ppermute | solution.py:185
  546.3 2.9 collective-permute-start.10
  571.5 8.0 %collective-permute-start.11 = (bf16[16,64,576]{2,1,0:T(8,128)(2,1)}, bf16[16,64,576]{2,1,0:T(8,128)(2,1)}, u32[]{:S(2)}, u32[]{:S(2)}) collective-permute-start(bf16[16,64,576]{2,1,0:T(8,128)(2,1)} %fusion.58), channel_id=1, source_target_pairs={{0,1},{1,0},{2,3},{3,2},{4,5},{5,4},{6,7},{7,6},{8,9},{9,8},{10,11... | collective-permute-start | bytes 3538952 | tf_op jit(solution)/shard_map/ppermute | solution.py:100
  579.2 7.0 collective-permute-start.12
  582.4 44.5 %all-to-all-start.7 = ((bf16[16,64,576]{2,1,0:T(8,128)(2,1)}), bf16[16,64,576]{2,1,0:T(8,128)(2,1)S(1)}, u32[]{:S(2)}, u32[]{:S(2)}) async-start(bf16[16,64,576]{2,1,0:T(8,128)(2,1)} %fusion.61), calls=%async_computation.11 | async-start | bytes 2621440 | tf_op jit(solution)/shard_map/all_to_all | solution.py:92
  586.1 135.0 %reduce-scatter.14.cloned.1.call-start = ((), (), s32[]{:S(2)}) async-start(), calls=%async_computation.23 | async-start | bytes 3440640 | tf_op jit(solution)/shard_map/reduce_scatter | solution.py:210
  588.3 26.1 %collective-permute-start.15 = (bf16[128,768]{1,0:T(8,128)(2,1)S(1)}, bf16[128,768]{1,0:T(8,128)(2,1)S(1)}, u32[]{:S(2)}, u32[]{:S(2)}) collective-permute-start(bf16[128,768]{1,0:T(8,128)(2,1)S(1)} %get-tuple-element.283), channel_id=1, source_target_pairs={{0,6},{2,4},{4,2},{6,0},{1,7},{3,5},{5,3},{7,1},{8,14},{10,12},{12... | collective-permute-start | bytes 589832 | tf_op jit(solution)/shard_map/ppermute | solution.py:176
  591.1 26.9 %collective-permute-start.14 = (bf16[128,768]{1,0:T(8,128)(2,1)S(1)}, bf16[128,768]{1,0:T(8,128)(2,1)S(1)}, u32[]{:S(2)}, u32[]{:S(2)}) collective-permute-start(bf16[128,768]{1,0:T(8,128)(2,1)S(1)} %get-tuple-element.284), channel_id=1, source_target_pairs={{0,4},{2,6},{4,0},{6,2},{1,5},{3,7},{5,1},{7,3},{8,12},{10,14},{12... | collective-permute-start | bytes 589832 | tf_op jit(solution)/shard_map/ppermute | solution.py:176
  591.6 28.2 %collective-permute-start.13 = (bf16[128,768]{1,0:T(8,128)(2,1)S(1)}, bf16[128,768]{1,0:T(8,128)(2,1)S(1)}, u32[]{:S(2)}, u32[]{:S(2)}) collective-permute-start(bf16[128,768]{1,0:T(8,128)(2,1)S(1)} %get-tuple-element.282), channel_id=1, source_target_pairs={{0,2},{2,0},{4,6},{6,4},{1,3},{3,1},{5,7},{7,5},{8,10},{10,8},{12,... | collective-permute-start | bytes 589832 | tf_op jit(solution)/shard_map/ppermute | solution.py:176
  619.9 6.9 collective-permute-start.16
  628.9 4.0 collective-permute-start.17
  654.0 28.5 %all-to-all-start.8 = ((bf16[16,64,144]{2,1,0:T(8,128)(2,1)}), bf16[16,64,144]{2,1,0:T(8,128)(2,1)S(1)}, u32[]{:S(2)}, u32[]{:S(2)}) async-start(bf16[16,64,144]{2,1,0:T(8,128)(2,1)} %bitcast.221), calls=%async_computation.12 | async-start | bytes 1048576 | tf_op jit(solution)/shard_map/all_to_all | solution.py:92
  686.4 7.7 %collective-permute-start.18 = (f32[72,2048]{1,0:T(8,128)}, f32[72,2048]{1,0:T(8,128)}, u32[]{:S(2)}, u32[]{:S(2)}) collective-permute-start(f32[72,2048]{1,0:T(8,128)} %constant_dynamic-slice_fusion), channel_id=1, source_target_pairs={{0,1},{1,0},{2,3},{3,2},{4,5},{5,4},{6,7},{7,6},{8,9},{9,8},{10,11... | collective-permute-start | bytes 1769480 | tf_op jit(solution)/shard_map/ppermute | solution.py:100
  696.1 25.0 %all-to-all-start.9 = ((bf16[16,91,128]{2,1,0:T(8,128)(2,1)}), bf16[16,91,128]{2,1,0:T(8,128)(2,1)S(1)}, u32[]{:S(2)}, u32[]{:S(2)}) async-start(bf16[16,91,128]{2,1,0:T(8,128)(2,1)} %pad_maximum_fusion.13), calls=%async_computation.13 | async-start | bytes 786432 | tf_op jit(solution)/shard_map/all_to_all | solution.py:92
  707.9 38.4 %reduce-scatter.12.cloned.1.call-start = ((), (), s32[]{:S(2)}) async-start(), calls=%async_computation.22 | async-start | bytes 1310720 | tf_op jit(solution)/shard_map/reduce_scatter | solution.py:158
  721.1 12.3 %all-to-all-start.10 = ((bf16[4,672,128]{2,1,0:T(8,128)(2,1)}), bf16[4,672,128]{2,1,0:T(8,128)(2,1)}, u32[]{:S(2)}, u32[]{:S(2)}) async-start(bf16[4,672,128]{2,1,0:T(8,128)(2,1)} %bitcast.271), calls=%async_computation.15 | async-start | bytes 1376256 | tf_op jit(solution)/shard_map/all_to_all | solution.py:92
  739.1 6.0 collective-permute-start.20
  746.3 1.9 collective-permute-start.19
  (136 other events, 1105.0 us)
Sparse Core Ops, SparseCore 0:
  12.5 164.5 all-gather.3
  180.6 100.1 all-gather.5
  284.2 77.6 all-gather.7
  414.2 81.7 reduce-scatter.5
  498.2 27.2 reduce-scatter.7
  528.8 92.4 reduce-scatter.9
  645.3 62.7 reduce-scatter.13
  717.7 28.5 reduce-scatter.11
where the time goes:
time: 764 us; the launch traced here: 756 us
  waiting for transfers between devices  335 us (44%)
  matrix products  187 us (24%)
  local copies, waits for them, and re-layouts  87 us (11%)
  starting transfers between devices  78.3 us (10%)
  other arithmetic  52.4 us (7%)
  between operations  16.9 us (2%)
    all_to_all x11, waiting for transfers between devices, exchange(): return lax.all_to_all(blocks, axes, split_axis=0, concat_axis=0, tiled=True)  152 us
    dot_general x14, matrix products, dot(): lax.dot_general(left_mat, right_mat, (((1,), (0,)), ((), ())), preferred_...  69.3 us
    all_to_all x11, starting transfers between devices, exchange(): return lax.all_to_all(blocks, axes, split_axis=0, concat_axis=0, tiled=True)  60.9 us
    dot_general x14, matrix products, dot_cols(): lax.dot_general(left_mat, right_mat, (((0,), (0,)), ((), ())), preferred_...  59 us
    dot_general x12, matrix products, dot_rows(): lax.dot_general(left_mat, right_mat, (((1,), (1,)), ((), ())), preferred_...  58.6 us
    all_gather x2, waiting for transfers between devices, gather_tokens(): return lax.all_gather(mine, ('plane', 'wt', 'line'), axis=0, tiled=True)  51.9 us
    ppermute x6, waiting for transfers between devices, group_sum(): own = own + lax.ppermute(block, 'plane', group_moves(k)).astype(F32)  50.6 us
    unnamed x311, local copies, waits for them, and re-layouts  35.8 us
  transfers between devices with their start and end apart: 40, of which 28 were waited for; matrix products, arithmetic and copies ran while one was open for 33% of the time, Pallas kernels for 0%

commit v1 on v0

--- a/solution.py
+++ b/solution.py
@@ -150,10 +150,15 @@
         return lax.all_gather(half_rows(values), CTX + ("wt",), axis=0, tiled=True)
 
     def gather_tokens(mine):
-        return lax.all_gather(mine, ("plane", "wt", "line"), axis=0, tiled=True)
+        return lax.all_gather(mine, ("plane", "line", "wt"), axis=0, tiled=True)
+
+    def wt_halves(left, right):
+        theirs = other_wt(dot_cols(left, right[0]).astype(BF16))
+        mine = lax.optimization_barrier(dot_cols(left, right[1]).astype(BF16))
+        return mine + theirs
 
     def scatter_tokens(values, beside=()):
-        some = lax.psum_scatter(values, ("plane", "wt"), scatter_dimension=0, tiled=True)
+        some = lax.psum_scatter(values, "plane", scatter_dimension=0, tiled=True)
         some, beside = lax.optimization_barrier((some, beside))
         return lax.psum_scatter(some, "line", scatter_dimension=0, tiled=True), beside
 
@@ -198,29 +203,36 @@
         blocks = jnp.broadcast_to(blocks[None], (groups,) + blocks.shape)
         return exchange(blocks.reshape((n,) + blocks.shape[2:])).reshape(-1, depth)
 
-    def from_head_groups(terms):
-        packed, shapes = [], []
+    lanes = 128
+
+    def pack_heads(terms):
+        packed = []
         for values in terms:
             k, depth = values.shape[0] // n, values.shape[1]
             split = values.astype(BF16).reshape(groups, group, k, depth // lanes, lanes)
             split = jnp.transpose(split, (0, 1, 3, 2, 4))
             packed.append(split.reshape(groups, group, -1, lanes))
-            shapes.append((k, depth // lanes))
-        packed = jnp.concatenate(packed, axis=2)
-        summed = lax.psum_scatter(
-            packed.reshape(-1, lanes), "line", scatter_dimension=0, tiled=True
-        )
-        got = exchange(summed.reshape(group, -1, lanes), "plane")
-
-        def finish(got):
-            out, at = [], 0
-            for k, blocks in shapes:
-                part = got[:, at : at + k * blocks].reshape(group, blocks, k, lanes)
-                out.append(jnp.transpose(part, (2, 0, 1, 3)).reshape(k, -1).astype(F32))
-                at += k * blocks
-            return out
-
-        return got, finish
+        return jnp.concatenate(packed, axis=2).reshape(-1, lanes)
+
+    def sum_packed(packed):
+        summed = lax.psum_scatter(packed, "line", scatter_dimension=0, tiled=True)
+        blocks = summed.reshape(group, -1, lanes)
+        own = lax.dynamic_index_in_dim(blocks, g, 0, keepdims=False)
+        out = lax.dynamic_update_index_in_dim(jnp.zeros_like(blocks), own, g, 0)
+        for k in range(1, group):
+            sent = lax.dynamic_index_in_dim(blocks, g ^ k, 0, keepdims=False)
+            got = lax.ppermute(sent, "plane", group_moves(k))
+            out = lax.dynamic_update_index_in_dim(out, got, g ^ k, 0)
+        return out
+
+    def unpack_heads(got, weights):
+        out, at = [], 0
+        for weight in weights:
+            k, blocks = weight.shape[0], weight.shape[1] // group // lanes
+            part = got[:, at : at + k * blocks].reshape(group, blocks, k, lanes)
+            out.append(jnp.transpose(part, (2, 0, 1, 3)).reshape(k, -1).astype(F32))
+            at += k * blocks
+        return out
 
     gains = exchange(
         jnp.broadcast_to(
@@ -239,19 +251,18 @@
     ff_own = shared_gate.shape[1] // n
     shared_stack = jnp.stack([shared_gate, shared_up, shared_down], axis=0)
     shared_blocks = jnp.transpose(shared_stack.reshape(3, own_d, n, ff_own), (2, 0, 3, 1))
-    gathered, kv_up_heads, q_up_heads, out_heads, gains, late = lax.optimization_barrier(
+    gathered, kv_up_heads, q_up_heads, gains, late = lax.optimization_barrier(
         (
             gathered,
             to_head_group(kv_up),
             to_head_group(q_up),
-            to_head_group(out_proj),
             gains,
-            (half_rows(grad_output), shared_blocks),
+            (half_rows(grad_output), out_proj),
         )
     )
-    go_half, shared_late = late
+    go_half, out_late = late
     go_all = gather_tokens(go_half)
-    shared_got = exchange(shared_late)
+    out_heads = to_head_group(out_late)
     if rows == own_d:
         x_all, down_all = gathered[0][:, :width], gathered[0][:, width:]
     else:
@@ -300,7 +311,6 @@
         exacts.append(exact)
         attended.append(dot(exact.astype(BF16), kv_h[:, NOPE:]).astype(BF16))
     attention = jnp.concatenate(attended, axis=1)
-    attention, shared_got = lax.optimization_barrier((attention, shared_got))
 
     inputs = layer_input.astype(F32)
     hidden_one = inputs + group_sum(dot_rows(attention, out_heads))
@@ -316,15 +326,16 @@
     gates_low = (gates - gates_high.astype(F32)).astype(BF16)
     gates_pad = jnp.zeros((rows, -2 * experts % 128), BF16)
     sent_rows = jnp.concatenate([normed_two, gates_high, gates_low, gates_pad], axis=1)
-    sent_rows, go_all = lax.optimization_barrier((sent_rows, go_all))
+    sent_rows, go_all, shared_blocks = lax.optimization_barrier((sent_rows, go_all, shared_blocks))
     got_rows = gather_tokens(half_rows(sent_rows))
 
     e_gate, e_up = jnp.transpose(expert_gate[0]), jnp.transpose(routed_expert_up_weight[0])
     ff = e_gate.shape[0]
     ff_all = ff + ff_own
+    shared_got = exchange(shared_blocks)
     s_gate, s_up, s_down = jnp.transpose(shared_got, (1, 2, 0, 3)).reshape(3, ff_own, width)
     mats = jnp.concatenate([e_gate, s_gate, e_up, s_up, expert_down[0], s_down], axis=0)
-    back_unit = dot_rows(go_all, mats[2 * ff_all :])
+    back_unit = dot_rows(mats[2 * ff_all :], go_all)
     normed_f, inverse_one = normalize(inputs, norm1_full)
     normed = normed_f.astype(BF16)
     q_latent = dot(normed, q_down_all)
@@ -334,40 +345,48 @@
     normed_half = lax.dynamic_index_in_dim(
         normed_all.reshape(n, wt, rows // wt, width), w, 1, keepdims=False
     ).reshape(tokens // wt, width)
+    cols = width // wt
+    mats_theirs = lax.dynamic_slice_in_dim(mats, (1 - w) * cols, cols, 1)
+    mats_mine = lax.dynamic_slice_in_dim(mats, w * cols, cols, 1)
     ready = (mats, back_unit, inverse_one, q_latent, q_inverse, kv_latent, kv_inverse, normed_half)
-    got_rows, ready = lax.optimization_barrier((got_rows, ready))
+    got_rows, ready, mats_theirs, mats_mine = lax.optimization_barrier(
+        (got_rows, ready, mats_theirs, mats_mine)
+    )
     mats, back_unit, inverse_one, q_latent, q_inverse, kv_latent, kv_inverse, normed_half = ready
     normed_two_all = got_rows[:, :width]
     got_gates = got_rows[:, width : width + 2 * experts].astype(F32)
     is_own = (jnp.arange(2 * experts) % experts == c)[None]
-    gate_own = jnp.sum(jnp.where(is_own, got_gates, 0.0), axis=-1, keepdims=True)
-
-    gate_pre = dot_rows(normed_two_all, mats[:ff_all])
-    up_pre = dot_rows(normed_two_all, mats[ff_all : 2 * ff_all])
+    gate_own = jnp.sum(jnp.where(is_own, got_gates, 0.0), axis=-1)[None]
+
+    gate_pre = dot_rows(mats[:ff_all], normed_two_all)
+    up_pre = dot_rows(mats[ff_all : 2 * ff_all], normed_two_all)
     act, slope = silu_parts(gate_pre)
     hidden = act * up_pre
-    is_expert = (jnp.arange(ff_all) < ff)[None]
+    is_expert = (jnp.arange(ff_all) < ff)[:, None]
     scale = jnp.where(is_expert, gate_own, 1.0)
     hidden_scaled = (hidden * scale).astype(BF16)
     back = back_unit * scale
     d_gate = (back * up_pre * slope).astype(BF16)
     d_up = (back * act).astype(BF16)
-    grad_gate_own = jnp.sum(jnp.where(is_expert, back_unit * hidden, 0.0), axis=-1)
-    d_normed = dot(jnp.concatenate([d_gate, d_up], axis=1), mats[: 2 * ff_all])
+    grad_gate_own = jnp.sum(jnp.where(is_expert, back_unit * hidden, 0.0), axis=0)
+    d_normed = wt_halves(
+        jnp.concatenate([d_gate, d_up], axis=0),
+        (mats_theirs[: 2 * ff_all], mats_mine[: 2 * ff_all]),
+    )
     d_normed, grad_gate_own, d_gate, d_up, hidden_scaled = lax.optimization_barrier(
-        (d_normed.astype(BF16), grad_gate_own, d_gate, d_up, hidden_scaled)
-    )
-    ffn_part = dot(hidden_scaled, mats[2 * ff_all :]).astype(BF16)
-    grad_expert_gate = dot_cols(d_gate[:, :ff], normed_two_all)
-    grad_expert_up = dot_cols(d_up[:, :ff], normed_two_all)
-    grad_expert_down = dot_cols(hidden_scaled[:, :ff], go_all)
-    grad_gates = wt_sum(grad_gate_own).reshape(group, wt, groups, rows // wt)
-    grad_gates = exchange(jnp.transpose(grad_gates, (2, 0, 1, 3)).reshape(n, rows))
+        (d_normed, grad_gate_own, d_gate, d_up, hidden_scaled)
+    )
+    ffn_part = wt_halves(hidden_scaled, (mats_theirs[2 * ff_all :], mats_mine[2 * ff_all :]))
+    grad_expert_gate = dot(d_gate[:ff], normed_two_all)
+    grad_expert_up = dot(d_up[:ff], normed_two_all)
+    grad_expert_down = dot(hidden_scaled[:ff], go_all)
+    grad_gates = wt_sum(grad_gate_own).reshape(group, groups, rows)
+    grad_gates = exchange(jnp.transpose(grad_gates, (1, 0, 2)).reshape(n, rows))
     grad_expert_gate = jnp.transpose(grad_expert_gate)[None]
     grad_expert_up = jnp.transpose(grad_expert_up)[None]
     grad_expert_down = grad_expert_down[None]
-    d_shared_in = dot_cols(jnp.concatenate([d_gate[:, ff:], d_up[:, ff:]], axis=1), normed_two_all)
-    d_shared_out = dot_cols(hidden_scaled[:, ff:], go_all)
+    d_shared_in = dot(jnp.concatenate([d_gate[ff:], d_up[ff:]], axis=0), normed_two_all)
+    d_shared_out = dot(hidden_scaled[ff:], go_all)
     d_shared = jnp.concatenate([d_shared_in, d_shared_out], axis=0).astype(BF16)
     d_shared = jnp.transpose(d_shared.reshape(3, ff_own, n, own_d), (2, 0, 1, 3))
     d_shared = exchange(d_shared)
@@ -377,8 +396,7 @@
     grad_normed_half, ffn_part, grad_expert_up, grad_expert_down = lax.optimization_barrier(
         (grad_normed_half, ffn_part, grad_expert_up, grad_expert_down)
     )
-    ffn_half = scatter_tokens(ffn_part)[0]
-    grad_normed_two = both_halves(grad_normed_half, 0).astype(F32)
+    grad_normed_two = both_halves(grad_normed_half, 1).astype(F32)
 
     grad_gates = jnp.where(picked, jnp.transpose(grad_gates), 0.0)
     grad_chosen = (
@@ -392,6 +410,8 @@
     grad_hidden = grad_hidden + upstream
     grad_hidden_half = grad_hidden.astype(BF16)
     hidden_group = group_gather(grad_hidden_half)
+    hidden_group, ffn_part = lax.optimization_barrier((hidden_group, ffn_part))
+    ffn_half = scatter_tokens(ffn_part)[0]
     grad_attention = dot(hidden_group, out_heads).astype(BF16)
 
     query_parts, kv_parts, rope_part = [], [], 0.0
@@ -414,21 +434,21 @@
     kv_part = kv_part.astype(BF16).reshape(n, wt, rows // wt, kvr + ROPE)
     kv_theirs = other_wt(lax.dynamic_index_in_dim(kv_part, 1 - w, 1, keepdims=False))
     kv_part = lax.dynamic_index_in_dim(kv_part, w, 1, keepdims=False) + kv_theirs
-    kv_got, grad_q_normed = lax.optimization_barrier(
-        (exchange(kv_part), group_sum(dot_rows(grad_query_half, q_up_heads)))
+    kv_got, grad_q_normed, packed = lax.optimization_barrier(
+        (
+            exchange(kv_part),
+            group_sum(dot_rows(grad_query_half, q_up_heads)),
+            pack_heads(
+                (
+                    dot_cols(hidden_group, attention),
+                    dot_cols(q_normed_group, grad_query_half),
+                    dot_cols(latent_all, grad_kv_heads),
+                )
+            ),
+        )
     )
     kv_own = both_halves(jnp.sum(kv_got.astype(F32), axis=0), 0)
-    weight_terms, kv_own = lax.optimization_barrier(
-        (
-            (
-                dot_cols(hidden_group, attention).astype(BF16),
-                dot_cols(q_normed_group, grad_query_half).astype(BF16),
-                dot_cols(latent_all, grad_kv_heads).astype(BF16),
-            ),
-            kv_own,
-        )
-    )
-    heads_back, heads_finish = from_head_groups(weight_terms)
+    heads_back = sum_packed(packed)
     d_shared = jnp.transpose(d_shared, (1, 3, 0, 2)).reshape(3, own_d, n * ff_own).astype(F32)
 
     grad_q_latent, qgain_part = norm_backward(grad_q_normed, q_latent, q_inverse, qgain_full)
@@ -442,10 +462,14 @@
     own_cols = -(-latents // (8 * n * wt)) * 8
     col_blocks = jnp.pad(half_rows(grad_latents), ((0, 0), (0, own_cols * n * wt - latents)))
     col_blocks = jnp.transpose(col_blocks.reshape(rows // wt, n, wt * own_cols), (1, 0, 2))
-    latent_cols = exchange(col_blocks).reshape(tokens // wt, wt * own_cols)
+    latent_cols = exchange(col_blocks)
     grad_normed = dot_rows(grad_latents, down_all[:, :latents])
     grad_input, norm1_part = norm_backward(grad_normed, inputs, inverse_one, norm1_full)
     grad_input = grad_input + grad_hidden
+    latent_cols, grad_input, norm1_part, d_shared = lax.optimization_barrier(
+        (latent_cols, grad_input, norm1_part, d_shared)
+    )
+    latent_cols = latent_cols.reshape(tokens // wt, wt * own_cols)
     down_cols = dot_cols(latent_cols, normed_half)
     down_theirs = other_wt(lax.dynamic_slice_in_dim(down_cols, (1 - w) * own_cols, own_cols, 0))
     down_cols = lax.dynamic_slice_in_dim(down_cols, w * own_cols, own_cols, 0) + down_theirs
@@ -463,13 +487,11 @@
     )
     last = jnp.concatenate([down_cols, small.reshape(n, -1, own_d)], axis=1)
     last = exchange(last.astype(BF16))
-    last, heads_back = lax.optimization_barrier((last, heads_back))
-    grad_out_proj, grad_q_up, grad_kv_up = heads_finish(heads_back)
-    last = last.astype(F32)
-    small = jnp.sum(last[:, own_cols:], axis=0).reshape(-1)
-    grad_down = both_halves(last[:, :own_cols], 1).reshape(-1, own_d)
+    grad_out_proj, grad_q_up, grad_kv_up = unpack_heads(heads_back, (out_proj, q_up, kv_up))
+    small = jnp.sum(last[:, own_cols:].astype(F32), axis=0).reshape(-1)
+    grad_down = both_halves(last[:, :own_cols], 1).reshape(-1, own_d).astype(F32)
     ffn_half = lax.optimization_barrier((ffn_half, last))[0]
-    output = (hidden_one + both_halves(ffn_half, 0).astype(F32)).astype(BF16)
+    output = (hidden_one + both_halves(ffn_half, 1).astype(F32)).astype(BF16)
     edge = 2 * own_d + own_q
     edge_kv = edge + kv_gain.shape[0]
     return (

time: 764 us -> 742 us (0.971)
  waiting for transfers between devices: 335 us -> 271 us
  local copies, waits for them, and re-layouts: 87 us -> 112 us
  other arithmetic: 52.4 us -> 74.8 us
  starting transfers between devices: 78.3 us -> 70.3 us
    all_to_all x11 -> x10, waiting for transfers between devices: 152 us -> 104 us  [exchange(): return lax.all_to_all(blocks, axes, split_axis=0, concat_axis=0, tiled=True)]
    all_gather x1, waiting for transfers between devices: 29.1 us -> 57.4 us  [gather_rows(): return lax.all_gather(half_rows(values), CTX + ('wt',), axis=0, tiled=True)]
    all_gather x2, waiting for transfers between devices: 51.9 us -> 31.3 us  [gather_tokens(): return lax.all_gather(mine, ('plane', 'line', 'wt'), axis=0, tiled=True)]
    reduce_scatter x3, waiting for transfers between devices: 21.4 us -> 1.69 us  [the longest x2 1.69 us: scatter_tokens(): some = lax.psum_scatter(values, 'plane', scatter_dimension=0, tiled=True)]
    ppermute x6, waiting for transfers between devices: 50.6 us -> 33.6 us  [group_sum(): own = own + lax.ppermute(block, 'plane', group_moves(k)).astype(F32)]
    add x0 -> x2, other arithmetic: none -> 10.6 us  [wt_halves(): return mine + theirs]
    reduce_scatter x2, waiting for transfers between devices: 9.21 us -> 19 us  [scatter_tokens(): lax.psum_scatter(some, 'line', scatter_dimension=0, tiled=True)]
    dynamic_slice x0 -> x1, local copies, waits for them, and re-layouts: none -> 8.86 us  [layer(): mats_mine = lax.dynamic_slice_in_dim(mats, w * cols, cols, 1)]
  transfers between devices with their start and end apart: 40 -> 44, of which waited for: 28 -> 28; matrix products, arithmetic and copies ran while one was open for 33% -> 40% of each run, Pallas kernels for 0% -> 0%
where the time goes in v1:
time: 742 us; the launch traced here: 735 us
  waiting for transfers between devices  271 us (37%)
  matrix products  190 us (26%)
  local copies, waits for them, and re-layouts  112 us (15%)
  other arithmetic  74.8 us (10%)
  starting transfers between devices  70.3 us (9%)
  between operations  17.1 us (2%)
    all_to_all x10, waiting for transfers between devices, exchange(): return lax.all_to_all(blocks, axes, split_axis=0, concat_axis=0, tiled=True)  104 us
    dot_general x17, matrix products, dot(): lax.dot_general(left_mat, right_mat, (((1,), (0,)), ((), ())), preferred_...  72.7 us
    dot_general x12, matrix products, dot_rows(): lax.dot_general(left_mat, right_mat, (((1,), (1,)), ((), ())), preferred_...  63.4 us
    all_gather x1, waiting for transfers between devices, gather_rows(): return lax.all_gather(half_rows(values), CTX + ('wt',), axis=0, tiled=True)  57.4 us
    dot_general x13, matrix products, dot_cols(): lax.dot_general(left_mat, right_mat, (((0,), (0,)), ((), ())), preferred_...  53.7 us
    all_to_all x10, starting transfers between devices, exchange(): return lax.all_to_all(blocks, axes, split_axis=0, concat_axis=0, tiled=True)  53.2 us
    unnamed x285, local copies, waits for them, and re-layouts  37 us
    ppermute x6, waiting for transfers between devices, group_sum(): own = own + lax.ppermute(block, 'plane', group_moves(k)).astype(F32)  33.6 us
  transfers between devices with their start and end apart: 44, of which 28 were waited for; matrix products, arithmetic and copies ran while one was open for 40% of the time, Pallas kernels for 0%

profile of v1, /device:TPU:0, one launch (start us, length us, event | category | flops | bytes accessed | tf_op | source)
XLA Modules:
  0.0 735.1 jit_solution(7624596553431959143)
XLA Ops:
  14.5 8.3 %all-to-all-start.2 = ((bf16[16,2,192]{2,1,0:T(2,128)(2,1)}), bf16[16,2,192]{2,1,0:T(2,128)(2,1)S(1)}, u32[]{:S(2)}, u32[]{:S(2)}) async-start(bf16[16,2,192]{2,1,0:T(2,128)(2,1)} %reshape.504), calls=%async_computation.2 | async-start | bytes 32768 | tf_op jit(solution)/shard_map/all_to_all | solution.py:92
  23.0 7.4 %all-to-all-done.2 = bf16[16,2,192]{2,1,0:T(2,128)(2,1)S(1)} async-done(((bf16[16,2,192]{2,1,0:T(2,128)(2,1)}), bf16[16,2,192]{2,1,0:T(2,128)(2,1)S(1)}, u32[]{:S(2)}, u32[]{:S(2)}) %all-to-all-start.2) | async-done | bytes 12320 | tf_op jit(solution)/shard_map/all_to_all | solution.py:92
  35.0 16.2 %all-to-all-done = bf16[16,32,512]{2,1,0:T(8,128)(2,1)S(1)} async-done(((bf16[16,32,512]{2,1,0:T(8,128)(2,1)}), bf16[16,32,512]{2,1,0:T(8,128)(2,1)S(1)}, u32[]{:S(2)}, u32[]{:S(2)}) %all-to-all-start) | async-done | bytes 524320 | tf_op jit(solution)/shard_map/all_to_all | solution.py:92
  52.4 4.3 all-to-all-start.1
  57.6 40.7 %all-to-all-done.1 = bf16[16,96,384]{2,1,0:T(8,128)(2,1)S(1)} async-done(((bf16[16,96,384]{2,1,0:T(8,128)(2,1)}), bf16[16,96,384]{2,1,0:T(8,128)(2,1)S(1)}, u32[]{:S(2)}, u32[]{:S(2)}) %all-to-all-start.1) | async-done | bytes 1179680 | tf_op jit(solution)/shard_map/all_to_all | solution.py:92
  98.3 57.4 %all-gather.4.cloned.1.call-done = bf16[2048,4224]{1,0:T(8,128)(2,1)} async-done(((bf16[64,4224]{1,0:T(8,128)(2,1)}), bf16[2048,4224]{1,0:T(8,128)(2,1)}) %all-gather.4.cloned.1.call-update) | async-done | bytes 17301520 | tf_op jit(solution)/shard_map/all_gather | solution.py:150
  161.3 5.1 fusion
  166.4 8.2 %fusion.2 = bf16[2048,2048]{1,0:T(8,128)(2,1)} fusion(f32[2048]{0:T(1024)S(1)} %get-tuple-element.321, f32[2048]{0:T(1024)S(1)} %add_rsqrt_fusion.1, bf16[2048,4224]{1,0:T(8,128)(2,1)} %all-gather.4.cloned.1.call-done), kind=kLoop, calls=%fused_computation.4 | loop fusion | flops 16777216 | bytes 16793600 | tf_op jit(solution)/shard_map/convert_element_type | solution.py:286
  174.9 6.5 multiply_reduce_fusion.1
  181.4 8.0 %fusion.46 = f32[2048,576]{0,1:T(8,128)S(1)} fusion(bf16[2048,2048]{1,0:T(8,128)(2,1)S(1)} %copy-done.2, bf16[2048,4224]{1,0:T(8,128)(2,1)} %all-gather.4.cloned.1.call-done), kind=kOutput, calls=%fused_computation.73 | convolution fusion | flops 4831838208 | bytes 15728640 | tf_op jit(solution)/shard_map/dot_general | solution.py:24
  214.4 12.0 %collective-permute-done.3 = bf16[128,1024]{1,0:T(8,128)(2,1)} collective-permute-done((bf16[128,1024]{1,0:T(8,128)(2,1)S(1)}, bf16[128,1024]{1,0:T(8,128)(2,1)}, u32[]{:S(2)}, u32[]{:S(2)}) %collective-permute-start.3) | collective-permute-done | bytes 262176 | tf_op jit(solution)/shard_map/ppermute | solution.py:181
  226.3 5.9 collective-permute-done.2
  232.2 5.7 collective-permute-done.1
  247.7 5.9 all-gather.6.cloned.1.call-done
  255.5 4.2 all-to-all-start.4
  263.6 4.9 constant_dynamic-slice_fusion.5
  272.3 4.7 multiply_reduce_fusion.7
  277.5 13.4 %all-to-all-done.4 = bf16[16,3,88,128]{3,2,1,0:T(8,128)(2,1)S(1)} async-done(((bf16[16,3,88,128]{3,2,1,0:T(8,128)(2,1)}), bf16[16,3,88,128]{3,2,1,0:T(8,128)(2,1)S(1)}, u32[]{:S(2)}, u32[]{:S(2)}) %all-to-all-start.4) | async-done | bytes 1081376 | tf_op jit(solution)/shard_map/all_to_all | solution.py:92
  298.3 8.9 %constant_dynamic-slice_fusion.3 = (bf16[2376,1024]{1,0:T(8,128)(2,1)}, bf16[2376,1024]{1,0:T(8,128)(2,1)}) fusion(bf16[2376,2048]{1,0:T(8,128)(2,1)} %constant_dynamic-update-slice_fusion, s32[]{:T(128)S(6)} %select_n.204, s32[]{:T(128)S(6)} %select_n.205), kind=kLoop, calls=%fused_computation.325 | loop fusion | bytes 19464200 | tf_op jit(solution)/shard_map/dynamic_slice | solution.py:350
  307.1 11.2 %fusion.33 = f32[792,2048]{1,0:T(8,128)} fusion(bf16[2048,2048]{1,0:T(8,128)(2,1)} %all-gather.6.cloned.1.call-done, bf16[88,2048]{1,0:T(8,128)(2,1)S(1)} %bitcast.294, bf16[704,2048]{1,0:T(8,128)(2,1)S(1)} %bitcast.276), kind=kOutput, calls=%fused_computation.51 | convolution fusion | flops 6650265600 | bytes 18120704 | tf_op jit(solution)/shard_map/dot_general | solution.py:30
  318.3 25.4 %all-gather.8.cloned.1.call-done = bf16[2048,2176]{1,0:T(8,128)(2,1)} async-done(((bf16[64,2176]{1,0:T(8,128)(2,1)}), bf16[2048,2176]{1,0:T(8,128)(2,1)}) %all-gather.8.cloned.1.call-update) | async-done | bytes 8912912 | tf_op jit(solution)/shard_map/all_gather | solution.py:153
  343.7 12.2 %fusion.17 = f32[792,2048]{1,0:T(8,128)} fusion(bf16[2048,2176]{1,0:T(8,128)(2,1)} %all-gather.8.cloned.1.call-done, bf16[2376,2048]{1,0:T(8,128)(2,1)} %constant_dynamic-update-slice_fusion), kind=kOutput, calls=%fused_computation.30 | convolution fusion | flops 6643777536 | bytes 18120704 | tf_op jit(solution)/shard_map/dot_general | solution.py:30
  357.1 18.7 %select_reduce_fusion = (f32[2048]{0:T(1024)S(1)}, bf16[792,2048]{1,0:T(8,128)(2,1)}, bf16[792,2048]{1,0:T(8,128)(2,1)}, bf16[792,2048]{1,0:T(8,128)(2,1)}) fusion(f32[792,2048]{1,0:T(8,128)} %fusion.33, pred[792]{0:T(1024)(128)(4,1)S(1)} %iota_compare_fusion.1, f32[792,2048]{1,0:T(8,128)} %fusion.17, f32[2048]{0:T(1024)S(1)} %select_reduce_fusion.1, ...), kind=kOutput, calls=%fused_computation.15 | convolution fusion | flops 6677837824 | bytes 34358040 | tf_op jit(solution)/shard_map/dot_general | solution.py:30
  375.9 11.4 %fusion.26 = bf16[2048,1024]{1,0:T(8,128)(2,1)S(1)} fusion(bf16[792,2048]{1,0:T(8,128)(2,1)} %get-tuple-element.78, bf16[792,2048]{1,0:T(8,128)(2,1)} %get-tuple-element.77, bf16[2376,1024]{1,0:T(8,128)(2,1)} %get-tuple-element.75), kind=kOutput, calls=%fused_computation.43 | convolution fusion | flops 6658850816 | bytes 13926400 | tf_op jit(solution)/shard_map/dot_general | solution.py:36
  387.6 8.4 %fusion.25 = bf16[2048,1024]{1,0:T(8,128)(2,1)S(1)} fusion(bf16[792,2048]{1,0:T(8,128)(2,1)S(1)} %copy-done.94, bf16[792,2048]{1,0:T(8,128)(2,1)S(1)} %copy-done.95, bf16[2376,1024]{1,0:T(8,128)(2,1)S(1)} %bitcast.263), kind=kOutput, calls=%fused_computation.42 | convolution fusion | flops 6658850816 | bytes 13926400 | tf_op jit(solution)/shard_map/dot_general | solution.py:36
  396.0 4.3 add.341
  402.2 8.0 %convolution_convert_fusion = bf16[2048,1024]{1,0:T(8,128)(2,1)} fusion(bf16[792,2048]{1,0:T(8,128)(2,1)S(1)} %copy-done.86, bf16[2376,1024]{1,0:T(8,128)(2,1)} %get-tuple-element.75), kind=kOutput, calls=%fused_computation.44 | convolution fusion | flops 3323985920 | bytes 9060352 | tf_op jit(solution)/shard_map/dot_general | solution.py:36
  413.1 5.8 fusion.48
  422.1 4.2 all-to-all-start.6
  427.9 5.6 all-to-all-done.6
  437.3 7.1 convolution_convert_fusion.1
  444.5 10.1 %fusion.30 = f32[1,2048,704]{1,2,0:T(8,128)} fusion(bf16[2048,2176]{1,0:T(8,128)(2,1)} %all-gather.8.cloned.1.call-done, bf16[792,2048]{1,0:T(8,128)(2,1)S(1)} %copy-done.96), kind=kOutput, calls=%fused_computation.47 | convolution fusion | flops 5905580032 | bytes 17039360 | tf_op jit(solution)/shard_map/dot_general | solution.py:24
  454.6 6.4 add.343
  463.0 11.3 %fusion.27 = f32[1,2048,704]{1,2,0:T(8,128)} fusion(bf16[2048,2176]{1,0:T(8,128)(2,1)} %all-gather.8.cloned.1.call-done, bf16[792,2048]{1,0:T(8,128)(2,1)} %get-tuple-element.78), kind=kOutput, calls=%fused_computation.46 | convolution fusion | flops 5905580032 | bytes 17039360 | tf_op jit(solution)/shard_map/dot_general | solution.py:24
  474.4 10.2 %convolution_bitcast_fusion = f32[1,704,2048]{2,1,0:T(8,128)} fusion(bf16[2048,2048]{1,0:T(8,128)(2,1)} %all-gather.6.cloned.1.call-done, bf16[792,2048]{1,0:T(8,128)(2,1)S(1)} %copy-done.87), kind=kOutput, calls=%fused_computation.48 | convolution fusion | flops 5905580032 | bytes 17039360 | tf_op jit(solution)/shard_map/dot_general | solution.py:24
  484.6 7.8 %reduce-scatter.8.cloned.1.call-done = bf16[128,1024]{1,0:T(8,128)(2,1)} async-done(((bf16[512,1024]{1,0:T(8,128)(2,1)}), bf16[128,1024]{1,0:T(8,128)(2,1)}) %reduce-scatter.8.cloned.1.call-update) | async-done | bytes 262160 | tf_op jit(solution)/shard_map/reduce_scatter | solution.py:163
  502.8 5.7 collective-permute-done.9
  509.3 5.2 collective-permute-done.10
  551.9 4.4 all-to-all-start.7
  556.4 5.6 convolution_convert_fusion.10
  575.7 4.3 reshape.474
  582.8 6.3 collective-permute-done.17
  627.6 5.7 all-to-all-start.8
  633.3 7.0 fusion.73
  641.7 14.5 %all-to-all-done.8 = bf16[16,64,144]{2,1,0:T(8,128)(2,1)} async-done(((bf16[16,64,144]{2,1,0:T(8,128)(2,1)}), bf16[16,64,144]{2,1,0:T(8,128)(2,1)}, u32[]{:S(2)}, u32[]{:S(2)}) %all-to-all-start.8) | async-done | bytes 294944 | tf_op jit(solution)/shard_map/all_to_all | solution.py:92
  665.7 10.7 %all-to-all-start.9 = ((bf16[16,91,128]{2,1,0:T(8,128)(2,1)}), bf16[16,91,128]{2,1,0:T(8,128)(2,1)}, u32[]{:S(2)}, u32[]{:S(2)}) async-start(bf16[16,91,128]{2,1,0:T(8,128)(2,1)} %pad_maximum_fusion.16), calls=%async_computation.13 | async-start | bytes 786432 | tf_op jit(solution)/shard_map/all_to_all | solution.py:92
  683.9 5.6 all-to-all-done.9
  709.2 11.2 %reduce-scatter.12.cloned.1.call-done = bf16[128,1024]{1,0:T(8,128)(2,1)} async-done(((bf16[512,1024]{1,0:T(8,128)(2,1)}), bf16[128,1024]{1,0:T(8,128)(2,1)}) %reduce-scatter.12.cloned.1.call-update) | async-done | bytes 262160 | tf_op jit(solution)/shard_map/reduce_scatter | solution.py:163
  (558 shorter events, 236.0 us)
Async XLA Ops:
  7.2 148.4 %all-gather.4.cloned.1.call-start = ((), (), s32[]{:S(2)}) async-start(), calls=%async_computation.15 | async-start | bytes 17842176 | tf_op jit(solution)/shard_map/all_gather | solution.py:150
  14.5 15.8 %all-to-all-start.2 = ((bf16[16,2,192]{2,1,0:T(2,128)(2,1)}), bf16[16,2,192]{2,1,0:T(2,128)(2,1)S(1)}, u32[]{:S(2)}, u32[]{:S(2)}) async-start(bf16[16,2,192]{2,1,0:T(2,128)(2,1)} %reshape.504), calls=%async_computation.2 | async-start | bytes 32768 | tf_op jit(solution)/shard_map/all_to_all | solution.py:92
  31.2 124.6 %copy-start.120 = (s32[16,2]{0,1:T(2,128)S(1)}, s32[16,2]{0,1:T(2,128)}, u32[]{:S(2)}) copy-start(s32[16,2]{0,1:T(2,128)} %param.21) | copy-start | bytes 388
  31.2 20.0 %all-to-all-start = ((bf16[16,32,512]{2,1,0:T(8,128)(2,1)}), bf16[16,32,512]{2,1,0:T(8,128)(2,1)S(1)}, u32[]{:S(2)}, u32[]{:S(2)}) async-start(bf16[16,32,512]{2,1,0:T(8,128)(2,1)} %bitcast.1), calls=%async_computation | async-start | bytes 1048576 | tf_op jit(solution)/shard_map/all_to_all | solution.py:92
  34.9 121.2 %copy-start.73 = (bf16[128,1024]{1,0:T(8,128)(2,1)S(1)}, bf16[128,1024]{1,0:T(8,128)(2,1)}, u32[]{:S(2)}) copy-start(bf16[128,1024]{1,0:T(8,128)(2,1)} %param.31) | copy-start | bytes 786436
  51.2 140.0 %copy-start.47 = (bf16[16,32,512]{2,1,0:T(8,128)(2,1)}, bf16[16,32,512]{2,1,0:T(8,128)(2,1)S(1)}, u32[]{:S(2)}) copy-start(bf16[16,32,512]{2,1,0:T(8,128)(2,1)S(1)} %all-to-all-done) | copy-start | bytes 1572868
  52.4 45.9 %all-to-all-start.1 = ((bf16[16,96,384]{2,1,0:T(8,128)(2,1)}), bf16[16,96,384]{2,1,0:T(8,128)(2,1)S(1)}, u32[]{:S(2)}, u32[]{:S(2)}) async-start(bf16[16,96,384]{2,1,0:T(8,128)(2,1)} %bitcast.4), calls=%async_computation.1 | async-start | bytes 2359296 | tf_op jit(solution)/shard_map/all_to_all | solution.py:92
  56.7 196.9 %all-gather.6.cloned.1.call-start = ((), (), s32[]{:S(2)}) async-start(), calls=%async_computation.16 | async-start | bytes 8650752 | tf_op jit(solution)/shard_map/all_gather | solution.py:153
  157.4 45.0 %all-to-all-start.3 = ((bf16[16,128,256]{2,1,0:T(8,128)(2,1)}), bf16[16,128,256]{2,1,0:T(8,128)(2,1)S(1)}, u32[]{:S(2)}, u32[]{:S(2)}) async-start(bf16[16,128,256]{2,1,0:T(8,128)(2,1)} %bitcast.8), calls=%async_computation.3 | async-start | bytes 2097152 | tf_op jit(solution)/shard_map/all_to_all | solution.py:92
  161.3 182.4 %all-gather.8.cloned.1.call-start = ((), (), s32[]{:S(2)}) async-start(), calls=%async_computation.17 | async-start | bytes 9191424 | tf_op jit(solution)/shard_map/all_gather | solution.py:153
  166.4 105.8 %copy-start.90 = (f32[2048]{0:T(1024)}, f32[2048]{0:T(1024)S(1)}, u32[]{:S(2)}) copy-start(f32[2048]{0:T(1024)S(1)} %get-tuple-element.321) | copy-start | bytes 24580
  206.0 2.7 collective-permute-start
  210.8 15.5 %collective-permute-start.3 = (bf16[128,1024]{1,0:T(8,128)(2,1)S(1)}, bf16[128,1024]{1,0:T(8,128)(2,1)}, u32[]{:S(2)}, u32[]{:S(2)}) collective-permute-start(bf16[128,1024]{1,0:T(8,128)(2,1)S(1)} %get-tuple-element.285), channel_id=1, source_target_pairs={{0,6},{2,4},{4,2},{6,0},{1,7},{3,5},{5,3},{7,1},{8,14},{10,12},{12... | collective-permute-start | bytes 786440 | tf_op jit(solution)/shard_map/ppermute | solution.py:181
  213.7 18.6 %collective-permute-start.2 = (bf16[128,1024]{1,0:T(8,128)(2,1)S(1)}, bf16[128,1024]{1,0:T(8,128)(2,1)}, u32[]{:S(2)}, u32[]{:S(2)}) collective-permute-start(bf16[128,1024]{1,0:T(8,128)(2,1)S(1)} %get-tuple-element.286), channel_id=1, source_target_pairs={{0,4},{2,6},{4,0},{6,2},{1,5},{3,7},{5,1},{7,3},{8,12},{10,14},{12... | collective-permute-start | bytes 786440 | tf_op jit(solution)/shard_map/ppermute | solution.py:181
  214.2 23.7 %collective-permute-start.1 = (bf16[128,1024]{1,0:T(8,128)(2,1)S(1)}, bf16[128,1024]{1,0:T(8,128)(2,1)}, u32[]{:S(2)}, u32[]{:S(2)}) collective-permute-start(bf16[128,1024]{1,0:T(8,128)(2,1)S(1)} %get-tuple-element.284), channel_id=1, source_target_pairs={{0,2},{2,0},{4,6},{6,4},{1,3},{3,1},{5,7},{7,5},{8,10},{10,8},{12,... | collective-permute-start | bytes 786440 | tf_op jit(solution)/shard_map/ppermute | solution.py:181
  239.2 3.0 collective-permute-start.4
  255.5 35.4 %all-to-all-start.4 = ((bf16[16,3,88,128]{3,2,1,0:T(8,128)(2,1)}), bf16[16,3,88,128]{3,2,1,0:T(8,128)(2,1)S(1)}, u32[]{:S(2)}, u32[]{:S(2)}) async-start(bf16[16,3,88,128]{3,2,1,0:T(8,128)(2,1)} %copy.269), calls=%async_computation.4 | async-start | bytes 2162688 | tf_op jit(solution)/shard_map/all_to_all | solution.py:92
  259.7 203.2 %reduce-scatter.6.cloned.1.call-start = ((), (), s32[]{:S(2)}) async-start(), calls=%async_computation.18 | async-start | bytes 5242880 | tf_op jit(solution)/shard_map/reduce_scatter | solution.py:161
  387.3 8.8 %collective-permute-start.5 = (bf16[2048,1024]{1,0:T(8,128)(2,1)S(1)}, bf16[2048,1024]{1,0:T(8,128)(2,1)S(1)}, u32[]{:S(2)}, u32[]{:S(2)}) collective-permute-start(bf16[2048,1024]{1,0:T(8,128)(2,1)S(1)} %fusion.26), channel_id=1, source_target_pairs={{0,1},{1,0},{2,3},{3,2},{4,5},{5,4},{6,7},{7,6},{8,9},{9,8},{10,11... | collective-permute-start | bytes 12582920 | tf_op jit(solution)/shard_map/ppermute | solution.py:100
  410.2 44.4 %collective-permute-start.7 = (bf16[2048,1024]{1,0:T(8,128)(2,1)}, bf16[2048,1024]{1,0:T(8,128)(2,1)}, u32[]{:S(2)}, u32[]{:S(2)}) collective-permute-start(bf16[2048,1024]{1,0:T(8,128)(2,1)} %convolution_convert_fusion), channel_id=1, source_target_pairs={{0,1},{1,0},{2,3},{3,2},{4,5},{5,4},{6,7},{7,6},{8,9},{9,8},{10,11... | collective-permute-start | bytes 12582920 | tf_op jit(solution)/shard_map/ppermute | solution.py:100
  412.8 8.7 %collective-permute-start.6 = (f32[2048]{0:T(1024)S(1)}, f32[2048]{0:T(1024)S(1)}, u32[]{:S(2)}, u32[]{:S(2)}) collective-permute-start(f32[2048]{0:T(1024)S(1)} %get-tuple-element.80), channel_id=1, source_target_pairs={{0,1},{1,0},{2,3},{3,2},{4,5},{5,4},{6,7},{7,6},{8,9},{9,8},{10,11... | collective-permute-start | bytes 24584 | tf_op jit(solution)/shard_map/ppermute | solution.py:100
  422.1 11.5 %all-to-all-start.6 = ((f32[16,1,128]{2,1,0:T(1,128)}), f32[16,1,128]{2,1,0:T(1,128)S(1)}, u32[]{:S(2)}, u32[]{:S(2)}) async-start(f32[16,1,128]{2,1,0:T(1,128)} %bitcast.36), calls=%async_computation.7 | async-start | bytes 16384 | tf_op jit(solution)/shard_map/all_to_all | solution.py:92
  433.5 27.8 %all-to-all-start.5 = ((bf16[16,3,88,128]{3,2,1,0:T(8,128)(2,1)}), bf16[16,3,88,128]{3,2,1,0:T(8,128)(2,1)S(1)}, u32[]{:S(2)}, u32[]{:S(2)}) async-start(bf16[16,3,88,128]{3,2,1,0:T(8,128)(2,1)} %bitcast.243), calls=%async_computation.6 | async-start | bytes 2162688 | tf_op jit(solution)/shard_map/all_to_all | solution.py:92
  437.2 55.2 %reduce-scatter.8.cloned.1.call-start = ((), (), s32[]{:S(2)}) async-start(), calls=%async_computation.19 | async-start | bytes 1310720 | tf_op jit(solution)/shard_map/reduce_scatter | solution.py:163
  463.0 231.8 %reduce-scatter.10.cloned.1.call-start = ((), (), s32[]{:S(2)}) async-start(), calls=%async_computation.20 | async-start | bytes 5242880 | tf_op jit(solution)/shard_map/reduce_scatter | solution.py:161
  492.4 1.7 collective-permute-start.8
  499.4 9.2 %collective-permute-start.9 = (bf16[128,1024]{1,0:T(8,128)(2,1)S(1)}, bf16[128,1024]{1,0:T(8,128)(2,1)S(1)}, u32[]{:S(2)}, u32[]{:S(2)}) collective-permute-start(bf16[128,1024]{1,0:T(8,128)(2,1)S(1)} %get-tuple-element.266), channel_id=1, source_target_pairs={{0,2},{2,0},{4,6},{6,4},{1,3},{3,1},{5,7},{7,5},{8,10},{10,8},{12,... | collective-permute-start | bytes 786440 | tf_op jit(solution)/shard_map/ppermute | solution.py:190
  500.8 13.7 %collective-permute-start.10 = (bf16[128,1024]{1,0:T(8,128)(2,1)S(1)}, bf16[128,1024]{1,0:T(8,128)(2,1)S(1)}, u32[]{:S(2)}, u32[]{:S(2)}) collective-permute-start(bf16[128,1024]{1,0:T(8,128)(2,1)S(1)} %get-tuple-element.266), channel_id=1, source_target_pairs={{0,4},{2,6},{4,0},{6,2},{1,5},{3,7},{5,1},{7,3},{8,12},{10,14},{12... | collective-permute-start | bytes 786440 | tf_op jit(solution)/shard_map/ppermute | solution.py:190
  502.3 12.9 %collective-permute-start.11 = (bf16[128,1024]{1,0:T(8,128)(2,1)S(1)}, bf16[128,1024]{1,0:T(8,128)(2,1)S(1)}, u32[]{:S(2)}, u32[]{:S(2)}) collective-permute-start(bf16[128,1024]{1,0:T(8,128)(2,1)S(1)} %get-tuple-element.266), channel_id=1, source_target_pairs={{0,6},{2,4},{4,2},{6,0},{1,7},{3,5},{5,3},{7,1},{8,14},{10,12},{12... | collective-permute-start | bytes 786440 | tf_op jit(solution)/shard_map/ppermute | solution.py:190
  516.0 3.0 collective-permute-start.12
  541.8 8.6 %collective-permute-start.13 = (bf16[16,64,576]{2,1,0:T(8,128)(2,1)S(1)}, bf16[16,64,576]{2,1,0:T(8,128)(2,1)S(1)}, u32[]{:S(2)}, u32[]{:S(2)}) collective-permute-start(bf16[16,64,576]{2,1,0:T(8,128)(2,1)S(1)} %fusion.60), channel_id=1, source_target_pairs={{0,1},{1,0},{2,3},{3,2},{4,5},{5,4},{6,7},{7,6},{8,9},{9,8},{10,11... | collective-permute-start | bytes 3538952 | tf_op jit(solution)/shard_map/ppermute | solution.py:100
  550.2 15.9 %collective-permute-start.14 = (bf16[512,768]{1,0:T(8,128)(2,1)}, bf16[512,768]{1,0:T(8,128)(2,1)}, u32[]{:S(2)}, u32[]{:S(2)}) collective-permute-start(bf16[512,768]{1,0:T(8,128)(2,1)} %dynamic-slice_convert_fusion.1), channel_id=1, source_target_pairs={{0,1},{1,0},{2,3},{3,2},{4,5},{5,4},{6,7},{7,6},{8,9},{9,8},{10,11... | collective-permute-start | bytes 2359304 | tf_op jit(solution)/shard_map/ppermute | solution.py:100
  551.9 54.0 %all-to-all-start.7 = ((bf16[16,64,576]{2,1,0:T(8,128)(2,1)}), bf16[16,64,576]{2,1,0:T(8,128)(2,1)}, u32[]{:S(2)}, u32[]{:S(2)}) async-start(bf16[16,64,576]{2,1,0:T(8,128)(2,1)} %fusion.63), calls=%async_computation.11 | async-start | bytes 2621440 | tf_op jit(solution)/shard_map/all_to_all | solution.py:92
  556.3 139.8 %reduce-scatter.14.cloned.1.call-start = ((), (), s32[]{:S(2)}) async-start(), calls=%async_computation.22 | async-start | bytes 3440640 | tf_op jit(solution)/shard_map/reduce_scatter | solution.py:218
  569.9 19.2 %collective-permute-start.17 = (bf16[128,768]{1,0:T(8,128)(2,1)}, bf16[128,768]{1,0:T(8,128)(2,1)}, u32[]{:S(2)}, u32[]{:S(2)}) collective-permute-start(bf16[128,768]{1,0:T(8,128)(2,1)} %get-tuple-element.290), channel_id=1, source_target_pairs={{0,6},{2,4},{4,2},{6,0},{1,7},{3,5},{5,3},{7,1},{8,14},{10,12},{12... | collective-permute-start | bytes 589832 | tf_op jit(solution)/shard_map/ppermute | solution.py:181
  572.6 19.7 %collective-permute-start.16 = (bf16[128,768]{1,0:T(8,128)(2,1)}, bf16[128,768]{1,0:T(8,128)(2,1)}, u32[]{:S(2)}, u32[]{:S(2)}) collective-permute-start(bf16[128,768]{1,0:T(8,128)(2,1)} %get-tuple-element.291), channel_id=1, source_target_pairs={{0,4},{2,6},{4,0},{6,2},{1,5},{3,7},{5,1},{7,3},{8,12},{10,14},{12... | collective-permute-start | bytes 589832 | tf_op jit(solution)/shard_map/ppermute | solution.py:181
  573.1 19.7 %collective-permute-start.15 = (bf16[128,768]{1,0:T(8,128)(2,1)}, bf16[128,768]{1,0:T(8,128)(2,1)}, u32[]{:S(2)}, u32[]{:S(2)}) collective-permute-start(bf16[128,768]{1,0:T(8,128)(2,1)} %get-tuple-element.289), channel_id=1, source_target_pairs={{0,2},{2,0},{4,6},{6,4},{1,3},{3,1},{5,7},{7,5},{8,10},{10,8},{12,... | collective-permute-start | bytes 589832 | tf_op jit(solution)/shard_map/ppermute | solution.py:181
  595.0 8.8 %collective-permute-start.18 = (f32[128,768]{1,0:T(8,128)}, f32[128,768]{1,0:T(8,128)}, u32[]{:S(2)}, u32[]{:S(2)}) collective-permute-start(f32[128,768]{1,0:T(8,128)} %fusion.93), channel_id=1, source_target_pairs={{0,1},{1,0},{2,3},{3,2},{4,5},{5,4},{6,7},{7,6},{8,9},{9,8},{10,11... | collective-permute-start | bytes 1179656 | tf_op jit(solution)/shard_map/ppermute | solution.py:100
  609.2 4.5 collective-permute-start.19
  627.6 28.7 %all-to-all-start.8 = ((bf16[16,64,144]{2,1,0:T(8,128)(2,1)}), bf16[16,64,144]{2,1,0:T(8,128)(2,1)}, u32[]{:S(2)}, u32[]{:S(2)}) async-start(bf16[16,64,144]{2,1,0:T(8,128)(2,1)} %bitcast.277), calls=%async_computation.12 | async-start | bytes 1048576 | tf_op jit(solution)/shard_map/all_to_all | solution.py:92
  661.3 2.3 collective-permute-start.20
  665.7 23.7 %all-to-all-start.9 = ((bf16[16,91,128]{2,1,0:T(8,128)(2,1)}), bf16[16,91,128]{2,1,0:T(8,128)(2,1)}, u32[]{:S(2)}, u32[]{:S(2)}) async-start(bf16[16,91,128]{2,1,0:T(8,128)(2,1)} %pad_maximum_fusion.16), calls=%async_computation.13 | async-start | bytes 786432 | tf_op jit(solution)/shard_map/all_to_all | solution.py:92
  676.5 43.9 %reduce-scatter.12.cloned.1.call-start = ((), (), s32[]{:S(2)}) async-start(), calls=%async_computation.21 | async-start | bytes 1310720 | tf_op jit(solution)/shard_map/reduce_scatter | solution.py:163
  690.4 3.2 collective-permute-start.22
  697.4 7.3 collective-permute-start.23
  698.8 10.2 %collective-permute-start.24 = (bf16[672,128]{1,0:T(8,128)(2,1)S(1)}, bf16[672,128]{1,0:T(8,128)(2,1)S(1)}, u32[]{:S(2)}, u32[]{:S(2)}) collective-permute-start(bf16[672,128]{1,0:T(8,128)(2,1)S(1)} %get-tuple-element.304), channel_id=1, source_target_pairs={{0,4},{2,6},{4,0},{6,2},{1,5},{3,7},{5,1},{7,3},{8,12},{10,14},{12... | collective-permute-start | bytes 516104 | tf_op jit(solution)/shard_map/ppermute | solution.py:224
  699.6 9.4 %collective-permute-start.25 = (bf16[672,128]{1,0:T(8,128)(2,1)S(1)}, bf16[672,128]{1,0:T(8,128)(2,1)S(1)}, u32[]{:S(2)}, u32[]{:S(2)}) collective-permute-start(bf16[672,128]{1,0:T(8,128)(2,1)S(1)} %get-tuple-element.303), channel_id=1, source_target_pairs={{0,6},{2,4},{4,2},{6,0},{1,7},{3,5},{5,3},{7,1},{8,14},{10,12},{12... | collective-permute-start | bytes 516104 | tf_op jit(solution)/shard_map/ppermute | solution.py:224
  720.4 5.5 collective-permute-start.21
  (127 other events, 1177.8 us)
Sparse Core Ops, SparseCore 0:
  12.5 143.1 all-gather.3
  159.2 94.3 all-gather.5
  257.1 86.5 all-gather.7
  400.5 62.4 reduce-scatter.5
  465.1 27.3 reduce-scatter.7
  522.3 71.9 reduce-scatter.9
  613.8 62.6 reduce-scatter.13
  694.9 25.4 reduce-scatter.11
